TPU v7x, 512 devices: a whole 4x4x16 slice. The times are simulated.
512 devices in a mesh: lon: 32 (over z_lo, y), lat: 4 (over x), ens: 4 (over z_hi, core).
Axes of the slice: x: 4, y: 4, z: 16 (z_hi: 2, z_lo: 8; z = z_hi * 8 + z_lo), core: 2. Of those that a mesh axis runs over, the one named last changes fastest.
Arguments:
- obs_values: bfloat16 [4, 32768, 256], P('ens', ('lon', 'lat')), may hold values from -6 to 6
- obs_tile: int32 [4, 32768, 1], P('ens', ('lon', 'lat')), may hold values from 0 to 127; in each aligned block of 256 rows (0 to 255, 256 to 511, ..., all dimensions but the last counted through in order) at most 4 rows name the same one
- obs_cell: int32 [4, 32768], P('ens', ('lon', 'lat')), may hold values from 0 to 255
- backdrop: bfloat16 [4, 32, 1024, 256], P('ens', 'lat', 'lon'), may hold values from -6 to 6
- seed_grad: bfloat16 [4, 32, 1024, 256], P('ens', 'lat', 'lon'), may hold values from -6 to 6
- kernels: float32 [4, 9, 256], replicated, may hold values from -1.5 to 1.5
- weights: bfloat16 [4, 256, 256], replicated, may hold values from -0.375 to 0.375
Outputs:
- state: bfloat16 [4, 32, 1024, 256], P('ens', 'lat', 'lon')
- weight_grad: float32 [4, 256, 256], replicated
- kernel_grad: float32 [4, 9, 256], replicated
- obs_grad: bfloat16 [4, 32768, 256], P('ens', ('lon', 'lat'))
Inputs may be any that keep to these rules, and one draw needn't show every extreme that they name: `obs_tile`: among the 256 observations of one device no tile is named more than 4 times, a bound that some block reaches.
All inputs are finite; a program needn't handle non-finite values.
Results may differ from a plain program's by a relative error of at most 0.012.
Values may be sent and summed in bfloat16 or wider, within the bound.
A program may use at most 64 MiB of HBM per device.

v0:
```python
import jax
import jax.numpy as jnp
from jax import lax
from jax.sharding import PartitionSpec as P


def with_halo(block, sides, width, periodic):
    for axis, dim in sides:
        count = lax.axis_size(axis)
        forward = [(i, i + 1) for i in range(count - 1)]
        if periodic:
            forward.append((count - 1, 0))
        backward = [(target, source) for source, target in forward]
        low = lax.ppermute(
            lax.slice_in_dim(block, block.shape[dim] - width, None, axis=dim), axis, forward
        )
        high = lax.ppermute(lax.slice_in_dim(block, 0, width, axis=dim), axis, backward)
        block = jnp.concatenate([low, block, high], axis=dim)
    return block


def rims(field):
    widened = with_halo(field, (("lat", 0),), 1, False)
    return with_halo(widened, (("lon", 1),), 1, True)


def depthwise(padded, kernel_rows, offset, sign):
    rows = padded.shape[0] - 2
    cols = padded.shape[1] - 2
    accum = jnp.zeros((rows, cols, padded.shape[2]), jnp.float32)
    for a in range(3):
        for b in range(3):
            row_off = offset + sign * a
            col_off = offset + sign * b
            accum = accum + kernel_rows[3 * a + b] * padded[
                row_off : row_off + rows, col_off : col_off + cols
            ].astype(jnp.float32)
    return accum


def on_device(obs_values, obs_tile, obs_cell, backdrop, seed_grad, kernels, weights):
    n_lon = lax.axis_size("lon")
    n_lat = lax.axis_size("lat")
    spatial = n_lon * n_lat
    obs_count = obs_values.shape[1]
    channels = obs_values.shape[2]
    slot_cap = 2 * obs_count // spatial
    lat_rows = backdrop.shape[1]
    lon_cols = backdrop.shape[2]
    n_cells = lat_rows * lon_cols
    n_layers = weights.shape[0]
    inv_scale = 1.0 / float(lax.axis_size("ens") * spatial * n_cells) ** 0.5
    target = obs_tile[0, :, 0]
    matches = target[:, None] == jnp.arange(spatial, dtype=jnp.int32)[None, :]
    running = jnp.cumsum(matches.astype(jnp.int32), axis=0)
    position = jnp.sum(running * matches.astype(jnp.int32), axis=1) - 1
    slot_of = target * slot_cap + position
    send_values = (
        jnp.zeros((spatial * slot_cap, channels), jnp.bfloat16).at[slot_of].set(obs_values[0])
    )
    send_cells = jnp.full((spatial * slot_cap,), -1, jnp.int32).at[slot_of].set(obs_cell[0])
    recv_values, recv_cells = (
        lax.all_to_all(
            send_values.reshape(1, spatial, slot_cap, channels),
            ("lon", "lat"),
            split_axis=1,
            concat_axis=0,
            tiled=True,
        ),
        lax.all_to_all(
            send_cells.reshape(1, spatial, slot_cap),
            ("lon", "lat"),
            split_axis=1,
            concat_axis=0,
            tiled=True,
        ),
    )
    recv_values = recv_values.reshape(spatial * slot_cap, channels)
    recv_cells = recv_cells.reshape(spatial * slot_cap)
    onehot_mask = recv_cells[None, :] == jnp.arange(n_cells, dtype=jnp.int32)[:, None]
    onehot = onehot_mask.astype(jnp.bfloat16)
    summed = jnp.dot(onehot, recv_values, preferred_element_type=jnp.float32)
    counts = jnp.sum(onehot_mask.astype(jnp.int32), axis=1)
    divisor = jnp.maximum(counts, 1).astype(jnp.float32)[:, None]
    hidden = (
        (backdrop[0].reshape(n_cells, channels).astype(jnp.float32) + summed / divisor)
        .astype(jnp.bfloat16)
        .reshape(lat_rows, lon_cols, channels)
    )
    pads, pre_acts, acts = ([], [], [])
    for layer_idx in range(n_layers):
        padded = rims(hidden)
        pre = depthwise(padded, kernels[layer_idx], 0, 1)
        act = jax.nn.silu(pre).astype(jnp.bfloat16)
        mixed = jnp.dot(
            act.reshape(n_cells, channels), weights[layer_idx], preferred_element_type=jnp.float32
        )
        hidden = (hidden.astype(jnp.float32) + mixed.reshape(lat_rows, lon_cols, channels)).astype(
            jnp.bfloat16
        )
        pads.append(padded)
        pre_acts.append(pre)
        acts.append(act)
    grad = seed_grad[0].astype(jnp.float32) * inv_scale
    wgrads = [None] * n_layers
    kgrads = [None] * n_layers
    for layer_idx in reversed(range(n_layers)):
        grad_bf = grad.astype(jnp.bfloat16).reshape(n_cells, channels)
        weight_part = lax.dot_general(
            acts[layer_idx].reshape(n_cells, channels),
            grad_bf,
            (((0,), (0,)), ((), ())),
            preferred_element_type=jnp.float32,
        )
        grad_act = lax.dot_general(
            grad_bf,
            weights[layer_idx],
            (((1,), (1,)), ((), ())),
            preferred_element_type=jnp.float32,
        )
        pre = pre_acts[layer_idx]
        sigma = jax.nn.sigmoid(pre)
        grad_pre = (
            grad_act.reshape(lat_rows, lon_cols, channels) * (sigma * (1.0 + pre * (1.0 - sigma)))
        ).astype(jnp.bfloat16)
        padded = pads[layer_idx]
        grad_wide = grad_pre.astype(jnp.float32)
        taps = []
        for a in range(3):
            for b in range(3):
                taps.append(
                    jnp.sum(
                        grad_wide * padded[a : a + lat_rows, b : b + lon_cols].astype(jnp.float32),
                        axis=(0, 1),
                    )
                )
        kernel_part = jnp.stack(taps)
        wgrads[layer_idx] = weight_part
        kgrads[layer_idx] = kernel_part
        grad = grad + depthwise(rims(grad_pre), kernels[layer_idx], 2, -1)
    weight_grad = jnp.stack(wgrads)
    kernel_grad = jnp.stack(kgrads)
    weight_grad, kernel_grad = lax.psum((weight_grad, kernel_grad), ("lon", "lat", "ens"))
    cell_grad = (grad.reshape(n_cells, channels) / divisor).astype(jnp.bfloat16)
    slot_grad = lax.dot_general(
        onehot, cell_grad, (((0,), (0,)), ((), ())), preferred_element_type=jnp.float32
    ).astype(jnp.bfloat16)
    returned = lax.all_to_all(
        slot_grad.reshape(spatial, 1, slot_cap, channels),
        ("lon", "lat"),
        split_axis=0,
        concat_axis=1,
        tiled=True,
    )
    obs_grad = returned.reshape(spatial * slot_cap, channels)[slot_of]
    return (hidden[None], weight_grad, kernel_grad, obs_grad[None])


def solution(mesh):
    placed = (
        P("ens", ("lon", "lat"), None),
        P("ens", ("lon", "lat"), None),
        P("ens", ("lon", "lat")),
        P("ens", "lat", "lon", None),
        P("ens", "lat", "lon", None),
        P(),
        P(),
    )
    return jax.shard_map(
        on_device,
        mesh=mesh,
        in_specs=placed,
        out_specs=(P("ens", "lat", "lon", None), P(), P(), P("ens", ("lon", "lat"), None)),
        check_vma=False,
    )
```

profile of v0, /device:TPU:1, one launch (start us, length us, event | category | flops | bytes accessed | tf_op | source)
XLA Modules:
  0.0 779.8 jit_solution(3772526640596903319)
XLA Ops:
  8.5 1.6 scatter_custom_fusion
  10.8 20.4 %all-to-all-start = ((s32[1,128,4]{2,0,1:T(1,128)}), s32[1,128,4]{2,0,1:T(1,128)S(1)}, u32[]{:S(2)}, u32[]{:S(2)}) async-start(s32[1,128,4]{2,0,1:T(1,128)} %bitcast.10), calls=%async_computation | async-start | bytes 131072 | tf_op jit(solution)/shard_map/all_to_all | solution.py:70
  31.2 1.5 scatter_custom_fusion.1
  33.5 11.0 %all-to-all-done = s32[1,128,4]{2,0,1:T(1,128)S(1)} async-done(((s32[1,128,4]{2,0,1:T(1,128)}), s32[1,128,4]{2,0,1:T(1,128)S(1)}, u32[]{:S(2)}, u32[]{:S(2)}) %all-to-all-start) | async-done | bytes 2080 | tf_op jit(solution)/shard_map/all_to_all | solution.py:70
  44.6 6.2 all-to-all-start.1
  52.3 16.1 %all-to-all-done.1 = bf16[1,128,4,256]{3,2,0,1:T(4,128)(2,1)S(1)} async-done(((bf16[1,128,4,256]{3,2,0,1:T(4,128)(2,1)}), bf16[1,128,4,256]{3,2,0,1:T(4,128)(2,1)S(1)}, u32[]{:S(2)}, u32[]{:S(2)}) %all-to-all-start.1) | async-done | bytes 262176 | tf_op jit(solution)/shard_map/all_to_all | solution.py:63
  68.8 2.4 collective-permute-start
  72.5 3.2 collective-permute-done.1
  75.8 3.6 collective-permute-start.2
  79.4 10.4 %collective-permute-start.3 = (bf16[10,1,256]{2,1,0:T(2,128)(2,1)S(1)}, bf16[10,1,256]{2,1,0:T(2,128)(2,1)S(1)}, u32[]{:S(2)}, u32[]{:S(2)}) collective-permute-start(bf16[10,1,256]{2,1,0:T(2,128)(2,1)S(1)} %get-tuple-element.106), channel_id=1, source_target_pairs={{16,0},{32,16},{48,32},{64,48},{80,64},{96,80},{112,96},{128,112},... | collective-permute-start | bytes 15368 | tf_op jit(solution)/shard_map/ppermute | solution.py:17
  91.9 4.3 collective-permute-start.4
  97.6 3.2 collective-permute-done.5
  100.8 1.9 collective-permute-start.6
  102.7 12.3 %collective-permute-start.7 = (bf16[10,1,256]{2,1,0:T(2,128)(2,1)S(1)}, bf16[10,1,256]{2,1,0:T(2,128)(2,1)S(1)}, u32[]{:S(2)}, u32[]{:S(2)}) collective-permute-start(bf16[10,1,256]{2,1,0:T(2,128)(2,1)S(1)} %get-tuple-element.102), channel_id=1, source_target_pairs={{16,0},{32,16},{48,32},{64,48},{80,64},{96,80},{112,96},{128,112},... | collective-permute-start | bytes 15368 | tf_op jit(solution)/shard_map/ppermute | solution.py:17
  116.4 3.1 collective-permute-start.8
  120.7 3.2 collective-permute-done.9
  123.9 1.9 collective-permute-start.10
  125.9 12.3 %collective-permute-start.11 = (bf16[10,1,256]{2,1,0:T(2,128)(2,1)S(1)}, bf16[10,1,256]{2,1,0:T(2,128)(2,1)S(1)}, u32[]{:S(2)}, u32[]{:S(2)}) collective-permute-start(bf16[10,1,256]{2,1,0:T(2,128)(2,1)S(1)} %get-tuple-element.98), channel_id=1, source_target_pairs={{16,0},{32,16},{48,32},{64,48},{80,64},{96,80},{112,96},{128,112},... | collective-permute-start | bytes 15368 | tf_op jit(solution)/shard_map/ppermute | solution.py:17
  139.5 2.1 collective-permute-start.12
  141.6 1.3 collective-permute-start.13
  143.0 3.5 collective-permute-done.13
  146.5 1.9 collective-permute-start.14
  148.4 12.3 %collective-permute-start.15 = (bf16[10,1,256]{2,1,0:T(2,128)(2,1)S(1)}, bf16[10,1,256]{2,1,0:T(2,128)(2,1)S(1)}, u32[]{:S(2)}, u32[]{:S(2)}) collective-permute-start(bf16[10,1,256]{2,1,0:T(2,128)(2,1)S(1)} %get-tuple-element.94), channel_id=1, source_target_pairs={{16,0},{32,16},{48,32},{64,48},{80,64},{96,80},{112,96},{128,112},... | collective-permute-start | bytes 15368 | tf_op jit(solution)/shard_map/ppermute | solution.py:17
  163.1 1.9 collective-permute-start.16
  166.3 3.5 collective-permute-done.17
  169.8 12.3 %collective-permute-start.18 = (bf16[10,1,256]{2,1,0:T(2,128)(2,1)S(1)}, bf16[10,1,256]{2,1,0:T(2,128)(2,1)S(1)}, u32[]{:S(2)}, u32[]{:S(2)}) collective-permute-start(bf16[10,1,256]{2,1,0:T(2,128)(2,1)S(1)} %get-tuple-element.89), channel_id=1, source_target_pairs={{16,0},{32,16},{48,32},{64,48},{80,64},{96,80},{112,96},{128,112},... | collective-permute-start | bytes 15368 | tf_op jit(solution)/shard_map/ppermute | solution.py:17
  182.1 1.9 collective-permute-start.19
  184.1 11.2 %collective-permute-done.19 = bf16[10,1,256]{2,1,0:T(2,128)(2,1)S(1)} collective-permute-done((bf16[10,1,256]{2,1,0:T(2,128)(2,1)S(1)}, bf16[10,1,256]{2,1,0:T(2,128)(2,1)S(1)}, u32[]{:S(2)}, u32[]{:S(2)}) %collective-permute-start.19) | collective-permute-done | bytes 5152 | tf_op jit(solution)/shard_map/ppermute | solution.py:14
  196.2 1.9 collective-permute-start.20
  199.4 3.2 collective-permute-done.21
  202.6 2.0 collective-permute-start.22
  204.6 3.5 collective-permute-start.23
  208.1 9.6 %collective-permute-done.23 = bf16[10,1,256]{2,1,0:T(2,128)(2,1)S(1)} collective-permute-done((bf16[10,1,256]{2,1,0:T(2,128)(2,1)S(1)}, bf16[10,1,256]{2,1,0:T(2,128)(2,1)S(1)}, u32[]{:S(2)}, u32[]{:S(2)}) %collective-permute-start.23) | collective-permute-done | bytes 5152 | tf_op jit(solution)/shard_map/ppermute | solution.py:14
  218.6 1.9 collective-permute-start.24
  221.8 3.2 collective-permute-done.25
  225.0 1.9 collective-permute-start.26
  226.9 3.4 collective-permute-start.27
  230.3 9.8 %collective-permute-done.27 = bf16[10,1,256]{2,1,0:T(2,128)(2,1)S(1)} collective-permute-done((bf16[10,1,256]{2,1,0:T(2,128)(2,1)S(1)}, bf16[10,1,256]{2,1,0:T(2,128)(2,1)S(1)}, u32[]{:S(2)}, u32[]{:S(2)}) %collective-permute-start.27) | collective-permute-done | bytes 5152 | tf_op jit(solution)/shard_map/ppermute | solution.py:14
  240.9 1.9 collective-permute-start.28
  244.5 2.9 collective-permute-done.29
  247.4 1.9 collective-permute-start.30
  249.3 3.4 collective-permute-start.31
  253.0 9.5 %collective-permute-done.31 = bf16[10,1,256]{2,1,0:T(2,128)(2,1)S(1)} collective-permute-done((bf16[10,1,256]{2,1,0:T(2,128)(2,1)S(1)}, bf16[10,1,256]{2,1,0:T(2,128)(2,1)S(1)}, u32[]{:S(2)}, u32[]{:S(2)}) %collective-permute-start.31) | collective-permute-done | bytes 5152 | tf_op jit(solution)/shard_map/ppermute | solution.py:14
  264.0 6.2 all-to-all-start.2
  272.9 126.5 %psum.15 = f32[4,9,256]{2,1,0:T(8,128)S(1)} all-reduce(f32[4,9,256]{2,1,0:T(8,128)S(1)} %pad_maximum_fusion.25), channel_id=1, replica_groups=mesh['lon'=32,'lat'=4,'ens'=4] {'lon','lat','ens'}, use_global_device_ids=true, to_apply=%region_43.44 | all-reduce | flops 9216 | bytes 73728 | tf_op jit(solution)/shard_map/psum | solution.py:143
  400.2 1.8 gather_fusion
  402.0 368.7 %all-reduce.2.cloned.1.call-done = f32[4,256,256]{2,1,0:T(8,128)} async-done(((f32[4,256,256]{2,1,0:T(8,128)}), f32[4,256,256]{2,1,0:T(8,128)}) %all-reduce.2.cloned.1.call-update) | async-done | bytes 1048592 | tf_op jit(solution)/shard_map/psum | solution.py:143
  770.7 2.3 copy.26
  (120 shorter events, 29.0 us)
Async XLA Ops:
  7.2 24.0 %copy-start = (bf16[1,256,256]{2,1,0:T(8,128)(2,1)S(1)}, bf16[1,256,256]{2,1,0:T(8,128)(2,1)}, u32[]{:S(2)}) copy-start(bf16[1,256,256]{2,1,0:T(8,128)(2,1)} %param.7) | copy-start | bytes 393220
  7.2 0.7 copy-start.3
  10.8 33.8 %all-to-all-start = ((s32[1,128,4]{2,0,1:T(1,128)}), s32[1,128,4]{2,0,1:T(1,128)S(1)}, u32[]{:S(2)}, u32[]{:S(2)}) async-start(s32[1,128,4]{2,0,1:T(1,128)} %bitcast.10), calls=%async_computation | async-start | bytes 131072 | tf_op jit(solution)/shard_map/all_to_all | solution.py:70
  44.6 23.9 %all-to-all-start.1 = ((bf16[1,128,4,256]{3,2,0,1:T(4,128)(2,1)}), bf16[1,128,4,256]{3,2,0,1:T(4,128)(2,1)S(1)}, u32[]{:S(2)}, u32[]{:S(2)}) async-start(bf16[1,128,4,256]{3,2,0,1:T(4,128)(2,1)} %reshape.215), calls=%async_computation.1 | async-start | bytes 524288 | tf_op jit(solution)/shard_map/all_to_all | solution.py:63
  52.3 16.2 %copy-start.5 = (bf16[1,8,32,256]{3,2,1,0:T(8,128)(2,1)S(1)}, bf16[1,8,32,256]{3,2,1,0:T(8,128)(2,1)}, u32[]{:S(2)}) copy-start(bf16[1,8,32,256]{3,2,1,0:T(8,128)(2,1)} %param.10) | copy-start | bytes 393220
  68.8 3.8 collective-permute-start
  71.2 4.5 collective-permute-start.1
  75.8 14.0 %copy-start.2 = (f32[4,9,256]{2,0,1:T(4,128)S(1)}, f32[4,9,256]{2,0,1:T(4,128)}, u32[]{:S(2)}) copy-start(f32[4,9,256]{2,0,1:T(4,128)} %param.12) | copy-start | bytes 110596
  75.8 14.1 %collective-permute-start.2 = (bf16[10,1,256]{2,1,0:T(2,128)(2,1)S(1)}, bf16[10,1,256]{2,1,0:T(2,128)(2,1)S(1)}, u32[]{:S(2)}, u32[]{:S(2)}) collective-permute-start(bf16[10,1,256]{2,1,0:T(2,128)(2,1)S(1)} %get-tuple-element.105), channel_id=1, source_target_pairs={{0,16},{16,32},{32,48},{48,64},{64,80},{80,96},{96,112},{112,128},... | collective-permute-start | bytes 15368 | tf_op jit(solution)/shard_map/ppermute | solution.py:14
  79.4 11.2 %collective-permute-start.3 = (bf16[10,1,256]{2,1,0:T(2,128)(2,1)S(1)}, bf16[10,1,256]{2,1,0:T(2,128)(2,1)S(1)}, u32[]{:S(2)}, u32[]{:S(2)}) collective-permute-start(bf16[10,1,256]{2,1,0:T(2,128)(2,1)S(1)} %get-tuple-element.106), channel_id=1, source_target_pairs={{16,0},{32,16},{48,32},{64,48},{80,64},{96,80},{112,96},{128,112},... | collective-permute-start | bytes 15368 | tf_op jit(solution)/shard_map/ppermute | solution.py:17
  90.7 1.0 copy-start.4
  91.9 5.6 collective-permute-start.4
  96.3 4.5 collective-permute-start.5
  100.8 14.3 %collective-permute-start.6 = (bf16[10,1,256]{2,1,0:T(2,128)(2,1)S(1)}, bf16[10,1,256]{2,1,0:T(2,128)(2,1)S(1)}, u32[]{:S(2)}, u32[]{:S(2)}) collective-permute-start(bf16[10,1,256]{2,1,0:T(2,128)(2,1)S(1)} %get-tuple-element.101), channel_id=1, source_target_pairs={{0,16},{16,32},{32,48},{48,64},{64,80},{80,96},{96,112},{112,128},... | collective-permute-start | bytes 15368 | tf_op jit(solution)/shard_map/ppermute | solution.py:14
  102.7 13.1 %collective-permute-start.7 = (bf16[10,1,256]{2,1,0:T(2,128)(2,1)S(1)}, bf16[10,1,256]{2,1,0:T(2,128)(2,1)S(1)}, u32[]{:S(2)}, u32[]{:S(2)}) collective-permute-start(bf16[10,1,256]{2,1,0:T(2,128)(2,1)S(1)} %get-tuple-element.102), channel_id=1, source_target_pairs={{16,0},{32,16},{48,32},{64,48},{80,64},{96,80},{112,96},{128,112},... | collective-permute-start | bytes 15368 | tf_op jit(solution)/shard_map/ppermute | solution.py:17
  116.4 4.4 collective-permute-start.8
  119.4 4.5 collective-permute-start.9
  123.9 14.3 %collective-permute-start.10 = (bf16[10,1,256]{2,1,0:T(2,128)(2,1)S(1)}, bf16[10,1,256]{2,1,0:T(2,128)(2,1)S(1)}, u32[]{:S(2)}, u32[]{:S(2)}) collective-permute-start(bf16[10,1,256]{2,1,0:T(2,128)(2,1)S(1)} %get-tuple-element.97), channel_id=1, source_target_pairs={{0,16},{16,32},{32,48},{48,64},{64,80},{80,96},{96,112},{112,128},... | collective-permute-start | bytes 15368 | tf_op jit(solution)/shard_map/ppermute | solution.py:14
  125.9 13.1 %collective-permute-start.11 = (bf16[10,1,256]{2,1,0:T(2,128)(2,1)S(1)}, bf16[10,1,256]{2,1,0:T(2,128)(2,1)S(1)}, u32[]{:S(2)}, u32[]{:S(2)}) collective-permute-start(bf16[10,1,256]{2,1,0:T(2,128)(2,1)S(1)} %get-tuple-element.98), channel_id=1, source_target_pairs={{16,0},{32,16},{48,32},{64,48},{80,64},{96,80},{112,96},{128,112},... | collective-permute-start | bytes 15368 | tf_op jit(solution)/shard_map/ppermute | solution.py:17
  139.5 3.4 collective-permute-start.12
  141.6 4.8 collective-permute-start.13
  146.5 14.3 %collective-permute-start.14 = (bf16[10,1,256]{2,1,0:T(2,128)(2,1)S(1)}, bf16[10,1,256]{2,1,0:T(2,128)(2,1)S(1)}, u32[]{:S(2)}, u32[]{:S(2)}) collective-permute-start(bf16[10,1,256]{2,1,0:T(2,128)(2,1)S(1)} %get-tuple-element.93), channel_id=1, source_target_pairs={{0,16},{16,32},{32,48},{48,64},{64,80},{80,96},{96,112},{112,128},... | collective-permute-start | bytes 15368 | tf_op jit(solution)/shard_map/ppermute | solution.py:14
  148.4 13.1 %collective-permute-start.15 = (bf16[10,1,256]{2,1,0:T(2,128)(2,1)S(1)}, bf16[10,1,256]{2,1,0:T(2,128)(2,1)S(1)}, u32[]{:S(2)}, u32[]{:S(2)}) collective-permute-start(bf16[10,1,256]{2,1,0:T(2,128)(2,1)S(1)} %get-tuple-element.94), channel_id=1, source_target_pairs={{16,0},{32,16},{48,32},{64,48},{80,64},{96,80},{112,96},{128,112},... | collective-permute-start | bytes 15368 | tf_op jit(solution)/shard_map/ppermute | solution.py:17
  161.6 0.9 copy-start.1
  163.1 3.2 collective-permute-start.16
  165.0 4.8 collective-permute-start.17
  169.8 14.3 %collective-permute-start.18 = (bf16[10,1,256]{2,1,0:T(2,128)(2,1)S(1)}, bf16[10,1,256]{2,1,0:T(2,128)(2,1)S(1)}, u32[]{:S(2)}, u32[]{:S(2)}) collective-permute-start(bf16[10,1,256]{2,1,0:T(2,128)(2,1)S(1)} %get-tuple-element.89), channel_id=1, source_target_pairs={{16,0},{32,16},{48,32},{64,48},{80,64},{96,80},{112,96},{128,112},... | collective-permute-start | bytes 15368 | tf_op jit(solution)/shard_map/ppermute | solution.py:17
  182.1 13.1 %collective-permute-start.19 = (bf16[10,1,256]{2,1,0:T(2,128)(2,1)S(1)}, bf16[10,1,256]{2,1,0:T(2,128)(2,1)S(1)}, u32[]{:S(2)}, u32[]{:S(2)}) collective-permute-start(bf16[10,1,256]{2,1,0:T(2,128)(2,1)S(1)} %get-tuple-element.90), channel_id=1, source_target_pairs={{0,16},{16,32},{32,48},{48,64},{64,80},{80,96},{96,112},{112,128},... | collective-permute-start | bytes 15368 | tf_op jit(solution)/shard_map/ppermute | solution.py:14
  196.2 3.2 collective-permute-start.20
  198.1 4.5 collective-permute-start.21
  202.6 5.5 collective-permute-start.22
  204.6 13.1 %collective-permute-start.23 = (bf16[10,1,256]{2,1,0:T(2,128)(2,1)S(1)}, bf16[10,1,256]{2,1,0:T(2,128)(2,1)S(1)}, u32[]{:S(2)}, u32[]{:S(2)}) collective-permute-start(bf16[10,1,256]{2,1,0:T(2,128)(2,1)S(1)} %get-tuple-element.86), channel_id=1, source_target_pairs={{0,16},{16,32},{32,48},{48,64},{64,80},{80,96},{96,112},{112,128},... | collective-permute-start | bytes 15368 | tf_op jit(solution)/shard_map/ppermute | solution.py:14
  218.6 3.2 collective-permute-start.24
  220.5 4.5 collective-permute-start.25
  225.0 5.3 collective-permute-start.26
  226.9 13.1 %collective-permute-start.27 = (bf16[10,1,256]{2,1,0:T(2,128)(2,1)S(1)}, bf16[10,1,256]{2,1,0:T(2,128)(2,1)S(1)}, u32[]{:S(2)}, u32[]{:S(2)}) collective-permute-start(bf16[10,1,256]{2,1,0:T(2,128)(2,1)S(1)} %get-tuple-element.82), channel_id=1, source_target_pairs={{0,16},{16,32},{32,48},{48,64},{64,80},{80,96},{96,112},{112,128},... | collective-permute-start | bytes 15368 | tf_op jit(solution)/shard_map/ppermute | solution.py:14
  240.9 3.5 collective-permute-start.28
  242.9 4.5 collective-permute-start.29
  247.4 5.6 collective-permute-start.30
  249.3 13.1 %collective-permute-start.31 = (bf16[10,1,256]{2,1,0:T(2,128)(2,1)S(1)}, bf16[10,1,256]{2,1,0:T(2,128)(2,1)S(1)}, u32[]{:S(2)}, u32[]{:S(2)}) collective-permute-start(bf16[10,1,256]{2,1,0:T(2,128)(2,1)S(1)} %get-tuple-element.78), channel_id=1, source_target_pairs={{0,16},{16,32},{32,48},{48,64},{64,80},{80,96},{96,112},{112,128},... | collective-permute-start | bytes 15368 | tf_op jit(solution)/shard_map/ppermute | solution.py:14
  264.0 136.1 %all-to-all-start.2 = ((bf16[128,1,4,256]{3,2,1,0:T(4,128)(2,1)}), bf16[128,1,4,256]{3,2,1,0:T(4,128)(2,1)S(1)}, u32[]{:S(2)}, u32[]{:S(2)}) async-start(bf16[128,1,4,256]{3,2,1,0:T(4,128)(2,1)} %bitcast.111), calls=%async_computation.2 | async-start | bytes 524288 | tf_op jit(solution)/shard_map/all_to_all | solution.py:148
  270.2 500.5 %all-reduce.2.cloned.1.call-start = ((), (), s32[]{:S(2)}) async-start(), calls=%async_computation.3 | async-start | bytes 2097152 | tf_op jit(solution)/shard_map/psum | solution.py:143
Sparse Core Ops, SparseCore 0:
  277.0 493.6 all-reduce.1
where the time goes:
time: 781 us; the launch traced here: 780 us
  waiting for transfers between devices  465 us (60%)
  starting transfers between devices  150 us (19%)
  blocking collectives  127 us (16%)
  between operations  14.8 us (2%)
  local copies, waits for them, and re-layouts  13.5 us (2%)
    psum x1, waiting for transfers between devices, on_device(): lax.psum((weight_grad, kernel_grad), ('lon', 'lat', 'ens'))  369 us
    psum x1, blocking collectives, on_device(): lax.psum((weight_grad, kernel_grad), ('lon', 'lat', 'ens'))  127 us
    ppermute x16, starting transfers between devices, with_halo(): lax.ppermute(lax.slice_in_dim(block, 0, width, axis=dim), axis, backward)  75.9 us
    ppermute x16, starting transfers between devices, with_halo(): lax.ppermute(lax.slice_in_dim(block, block.shape[dim] - width, None, axis...  41.1 us
    ppermute x16, waiting for transfers between devices, with_halo(): lax.ppermute(lax.slice_in_dim(block, block.shape[dim] - width, None, axis...  40.1 us
    ppermute x16, waiting for transfers between devices, with_halo(): lax.ppermute(lax.slice_in_dim(block, 0, width, axis=dim), axis, backward)  28.8 us
    all_to_all x1, starting transfers between devices, on_device(): lax.all_to_all(send_cells.reshape(1, spatial, slot_cap), ('lon', 'lat'),...  20.4 us
    all_to_all x1, waiting for transfers between devices, on_device(): lax.all_to_all(send_values.reshape(1, spatial, slot_cap, channels), ('lon...  16.1 us
  transfers between devices with their start and end apart: 36, of which 19 were waited for; matrix products, arithmetic and copies ran while one was open for 1% of the time, Pallas kernels for 0%

commit v1 on v0

v1 whole, which is shorter than its diff:
```python
import jax
import jax.numpy as jnp
from jax import lax
from jax.experimental import pallas as pl
from jax.experimental.pallas import tpu as pltpu
from jax.sharding import PartitionSpec as P

F32 = jnp.float32
BF16 = jnp.bfloat16
MESH = pl.DeviceIdType.MESH
NX, NY, NZL, NZH, NC = 4, 4, 8, 2, 2
NZ = NZL * NZH


def reduce_kernel(
    w_ref, k_ref, wo_ref, ko_ref,
    c_send, c_recv, x_send, x_recv, y_send, y_recv, z_send, z_recv,
    zg, yg, xg, cg,
    kc_recv, kx_send, kx_recv, ky_send, ky_recv, kyg, kxg,
    c_ss, c_rs, x_ss, x_rs, y_ss, y_rs, z_ss, z_rs, g_ss, g_rs,
    kc_ss, kc_rs, kx_ss, kx_rs, ky_ss, ky_rs, kyg_ss, kyg_rs, kxg_ss, kxg_rs,
    yg_ss, yg_rs, xg_ss, xg_rs, cg_ss, cg_rs,
):
    lon = lax.axis_index("lon")
    x = lax.axis_index("lat")
    ens = lax.axis_index("ens")
    zl, y = lon // NY, lon % NY
    zh, core = ens // NC, ens % NC
    z = zh * NZL + zl

    def at(px, py, pz, pc):
        return {"lon": (pz % NZL) * NY + py, "lat": px, "ens": (pz // NZL) * NC + pc}

    other = at(x, y, z, 1 - core)
    x_peers = [((x + k) % NX, k) for k in range(1, NX)]
    y_peers = [((y + k) % NY, k) for k in range(1, NY)]
    z_peers = [((z + k) % NZ, k) for k in range(1, NZ)]
    g_peers = [(zh * NZL + (zl + k) % NZL, k) for k in range(1, NZL)]

    barrier = pltpu.get_barrier_semaphore()
    greeted = [other]
    greeted += [at(p, y, z, core) for p, _ in x_peers]
    greeted += [at(x, p, z, core) for p, _ in y_peers]
    greeted += [at(x, y, p, core) for p, _ in z_peers]
    for peer in greeted:
        pl.semaphore_signal(barrier, inc=1, device_id=peer, device_id_type=MESH)
    pl.semaphore_wait(barrier, len(greeted))

    def copy(src, dst, ss, rs, peer):
        return pltpu.make_async_remote_copy(
            src_ref=src, dst_ref=dst, send_sem=ss, recv_sem=rs, device_id=peer, device_id_type=MESH
        )

    def go(copies):
        for c in copies:
            c.start()
        return copies

    def done(copies):
        for c in copies:
            c.wait()

    half = c_send.shape[1]
    for c in range(NC):
        c_send[c] = w_ref[c * half : (c + 1) * half].astype(BF16)
    live = go([
        copy(c_send.at[1 - core], c_recv, c_ss, c_rs, other),
        copy(k_ref, kc_recv, kc_ss, kc_rs, other),
    ])
    done(live)
    rows = x_send.shape[1]
    for p in range(NX):
        mine = w_ref[pl.ds(pl.multiple_of(core * half + p * rows, rows), rows)]
        x_send[p] = (mine + c_recv[p * rows : (p + 1) * rows].astype(F32)).astype(BF16)
    kx_send[...] = k_ref[...] + kc_recv[...]
    kx_recv[x] = kx_send[x]
    live = go(
        [copy(x_send.at[p], x_recv.at[x], x_ss.at[k], x_rs.at[k], at(p, y, z, core)) for p, k in x_peers]
        + [copy(kx_send.at[p], kx_recv.at[x], kx_ss.at[k], kx_rs.at[k], at(p, y, z, core)) for p, k in x_peers]
    )
    x_recv[x] = x_send[x]
    done(live)
    rows = y_send.shape[1]
    for p in range(NY):
        part = pl.ds(p * rows, rows)
        total = x_recv[0, part].astype(F32)
        for q in range(1, NX):
            total = total + x_recv[q, part].astype(F32)
        y_send[p] = total.astype(BF16)
    ksum = kx_recv[0] + kx_recv[1] + kx_recv[2] + kx_recv[3]
    for p in range(NY):
        ky_send[p] = ksum[(p // 2) * 8 : (p // 2) * 8 + 8, (p % 2) * 128 : (p % 2) * 128 + 128]
    live = go(
        [copy(y_send.at[p], y_recv.at[y], y_ss.at[k], y_rs.at[k], at(x, p, z, core)) for p, k in y_peers]
        + [copy(ky_send.at[p], ky_recv.at[y], ky_ss.at[k], ky_rs.at[k], at(x, p, z, core)) for p, k in y_peers]
    )
    y_recv[y] = y_send[y]
    ky_recv[y] = ky_send[y]
    done(live)
    total = y_recv[0].astype(F32)
    for q in range(1, NY):
        total = total + y_recv[q].astype(F32)
    ktile = ky_recv[0] + ky_recv[1] + ky_recv[2] + ky_recv[3]
    for p in range(NZL):
        z_send[p, 0] = total[(p // 2) * 8 : (p // 2) * 8 + 8, (p % 2) * 128 : (p % 2) * 128 + 128]
        z_send[p, 1] = ktile
    live = go([
        copy(z_send.at[p % NZL], z_recv.at[z], z_ss.at[k], z_rs.at[k], at(x, y, p, core)) for p, k in z_peers
    ])
    z_recv[z] = z_send[zl]
    done(live)
    both = z_recv[0]
    for q in range(1, NZ):
        both = both + z_recv[q]
    zg[zl] = both[0]
    kyg[y] = both[1]
    live = go([copy(zg.at[zl], zg.at[zl], g_ss.at[k], g_rs.at[k], at(x, y, p, core)) for p, k in g_peers])
    klive = go([
        copy(kyg.at[y], kyg.at[y], kyg_ss.at[k], kyg_rs.at[k], at(x, p, z, core)) for p, k in y_peers
    ])
    done(klive)
    kxg[x] = kyg[...]
    klive = go([
        copy(kyg, kxg.at[x], kxg_ss.at[k], kxg_rs.at[k], at(p, y, z, core)) for p, k in x_peers
    ])
    done(live)
    for p in range(NZL):
        r = (p // 2) * 8
        c = (p % 2) * 128
        y_send[0, r : r + 8, c : c + 128] = zg[p].astype(BF16)
    yg[y] = y_send[0]
    live = go([
        copy(y_send.at[0], yg.at[y], yg_ss.at[k], yg_rs.at[k], at(x, p, z, core)) for p, k in y_peers
    ])
    done(live)
    live = go([
        copy(yg, xg.at[x], xg_ss.at[k], xg_rs.at[k], at(p, y, z, core)) for p, k in x_peers
    ])
    xg[x] = yg[...]
    done(live)
    live = go([copy(xg, cg, cg_ss, cg_rs, other)])
    done(klive)
    for q in range(NX):
        for p in range(NY):
            r = (p // 2) * 8
            c = (p % 2) * 128
            ko_ref[q, r : r + 8, c : c + 128] = kxg[q, p]
    rows = yg.shape[1]
    for q in range(NX):
        for p in range(NY):
            lo = (q * NY + p) * rows
            wo_ref[pl.ds(pl.multiple_of(core * half + lo, rows), rows)] = xg[q, p].astype(F32)
    done(live)
    for q in range(NX):
        for p in range(NY):
            lo = (q * NY + p) * rows
            wo_ref[pl.ds(pl.multiple_of((1 - core) * half + lo, rows), rows)] = cg[q, p].astype(F32)


def reduce_params(wgrad, kgrad):
    layers, depth, channels = wgrad.shape
    taps = kgrad.shape[1]
    rows = layers * depth
    k_pad = jnp.pad(kgrad, ((0, 0), (0, 16 - taps), (0, 0)))
    rx, ry = rows // (NC * NX), rows // (NC * NX * NY)
    V = pltpu.VMEM
    D = pltpu.SemaphoreType.DMA
    w, k = pl.pallas_call(
        reduce_kernel,
        out_shape=(
            jax.ShapeDtypeStruct((rows, channels), F32),
            jax.ShapeDtypeStruct(k_pad.shape, F32),
        ),
        in_specs=[pl.BlockSpec(memory_space=V)] * 2,
        out_specs=(pl.BlockSpec(memory_space=V),) * 2,
        scratch_shapes=[
            V((NC, rows // NC, channels), BF16), V((rows // NC, channels), BF16),
            V((NX, rx, channels), BF16), V((NX, rx, channels), BF16),
            V((NY, ry, channels), BF16), V((NY, ry, channels), BF16),
            V((NZL, 2, 8, 128), F32), V((NZ, 2, 8, 128), F32),
            V((NZL, 8, 128), F32), V((NY, ry, channels), BF16),
            V((NX, NY, ry, channels), BF16), V((NX, NY, ry, channels), BF16),
            V(k_pad.shape, F32), V(k_pad.shape, F32), V(k_pad.shape, F32),
            V((NY, 8, 128), F32), V((NY, 8, 128), F32), V((NY, 8, 128), F32),
            V((NX, NY, 8, 128), F32),
            D, D, D((NX,)), D((NX,)), D((NY,)), D((NY,)), D((NZ,)), D((NZ,)), D((NZL,)), D((NZL,)),
            D, D, D((NX,)), D((NX,)), D((NY,)), D((NY,)), D((NY,)), D((NY,)), D((NX,)), D((NX,)),
            D((NY,)), D((NY,)), D((NX,)), D((NX,)), D, D,
        ],
        compiler_params=pltpu.CompilerParams(collective_id=0, has_side_effects=True),
        name="param_sum",
    )(wgrad.reshape(rows, channels), k_pad)
    return w.reshape(wgrad.shape), k[:, :taps]


def with_halo(block, sides, width):
    for axis, dim, periodic in sides:
        count = lax.axis_size(axis)
        forward = [(i, i + 1) for i in range(count - 1)]
        if periodic:
            forward.append((count - 1, 0))
        backward = [(target, source) for source, target in forward]
        low = lax.ppermute(
            lax.slice_in_dim(block, block.shape[dim] - width, None, axis=dim), axis, forward
        )
        high = lax.ppermute(lax.slice_in_dim(block, 0, width, axis=dim), axis, backward)
        block = jnp.concatenate([low, block, high], axis=dim)
    return block


SIDES = (("lat", 0, False), ("lon", 1, True))


def depthwise(padded, kernel_rows, offset, sign):
    rows = padded.shape[0] - 2
    cols = padded.shape[1] - 2
    accum = jnp.zeros((rows, cols, padded.shape[2]), F32)
    for a in range(3):
        for b in range(3):
            row_off = offset + sign * a
            col_off = offset + sign * b
            accum = accum + kernel_rows[3 * a + b] * padded[
                row_off : row_off + rows, col_off : col_off + cols
            ].astype(F32)
    return accum


def crop(v, n):
    if n == 0:
        return v
    return v[n : v.shape[0] - n, n : v.shape[1] - n]


def on_device(obs_values, obs_tile, obs_cell, backdrop, seed_grad, kernels, weights):
    n_lon = lax.axis_size("lon")
    n_lat = lax.axis_size("lat")
    spatial = n_lon * n_lat
    obs_count = obs_values.shape[1]
    channels = obs_values.shape[2]
    cap = 2 * obs_count // spatial
    lat_rows = backdrop.shape[1]
    lon_cols = backdrop.shape[2]
    n_cells = lat_rows * lon_cols
    n_layers = weights.shape[0]
    inv_scale = 1.0 / float(lax.axis_size("ens") * spatial * n_cells) ** 0.5

    def inside(v, radius):
        row = lax.broadcasted_iota(jnp.int32, (v.shape[0], 1, 1), 0)
        row = row + lax.axis_index("lat") * lat_rows - radius
        return jnp.where((row >= 0) & (row < n_lat * lat_rows), v, jnp.zeros((), v.dtype))

    seed_wide = with_halo(seed_grad[0], tuple(SIDES), n_layers)

    target = obs_tile[0, :, 0]
    matches = (target[:, None] == jnp.arange(spatial, dtype=jnp.int32)[None, :]).astype(BF16)
    order = jnp.arange(obs_count, dtype=jnp.int32)
    before = (order[:, None] > order[None, :]).astype(BF16)
    ahead = jnp.dot(before, matches, preferred_element_type=F32)
    position = jnp.sum(ahead * matches.astype(F32), axis=1).astype(jnp.int32)
    slot_of = target * cap + position
    place = (slot_of[:, None] == jnp.arange(spatial * cap, dtype=jnp.int32)[None, :]).astype(BF16)
    send_values = lax.dot_general(
        place, obs_values[0], (((0,), (0,)), ((), ())), preferred_element_type=F32
    ).astype(BF16)
    lane = jnp.arange(channels, dtype=jnp.int32)[None, :]
    cell_rows = jnp.where(position[:, None] == lane, obs_cell[0][:, None] + 1, 0).astype(BF16)
    send_cells = (
        lax.dot_general(matches, cell_rows, (((0,), (0,)), ((), ())), preferred_element_type=F32) - 1.0
    ).astype(BF16)
    packed = jnp.concatenate(
        [send_values.reshape(spatial, cap, channels), send_cells.reshape(spatial, 1, channels)], axis=1
    )
    got = lax.all_to_all(
        packed[None], ("lon", "lat"), split_axis=1, concat_axis=0, tiled=True
    ).reshape(spatial, cap + 1, channels)
    recv_values = got[:, :cap].reshape(spatial * cap, channels)
    recv_cells = got[:, cap, :cap].astype(jnp.int32).reshape(spatial * cap)
    onehot_mask = recv_cells[None, :] == jnp.arange(n_cells, dtype=jnp.int32)[:, None]
    onehot = onehot_mask.astype(BF16)
    summed = jnp.dot(onehot, recv_values, preferred_element_type=F32)
    counts = jnp.sum(onehot_mask.astype(jnp.int32), axis=1)
    divisor = jnp.maximum(counts, 1).astype(F32)[:, None]
    hidden = (
        (backdrop[0].reshape(n_cells, channels).astype(F32) + summed / divisor)
        .astype(BF16)
        .reshape(lat_rows, lon_cols, channels)
    )
    wide = 2 * n_layers
    hidden = with_halo(hidden, SIDES, wide)
    fields, pre_acts, acts = [], [], []
    for l in range(n_layers):
        radius = wide - 1 - l
        pre = depthwise(hidden, kernels[l], 0, 1)
        act = jax.nn.silu(pre).astype(BF16)
        mixed = jnp.dot(act.reshape(-1, channels), weights[l], preferred_element_type=F32)
        fields.append(crop(hidden, radius))
        pre_acts.append(crop(pre, radius - l - 1))
        acts.append(crop(act, radius).reshape(n_cells, channels))
        if l == n_layers - 1:
            act = crop(act, radius)
            mixed = jnp.dot(act.reshape(-1, channels), weights[l], preferred_element_type=F32)
            state = (crop(hidden, radius + 1).astype(F32) + mixed.reshape(lat_rows, lon_cols, channels)).astype(BF16)
        else:
            hidden = inside(
                (crop(hidden, 1).astype(F32) + mixed.reshape(pre.shape)).astype(BF16), radius
            )
    grad = seed_wide.astype(F32) * inv_scale
    wgrads = [None] * n_layers
    kgrads = [None] * n_layers
    for l in reversed(range(n_layers)):
        radius = l + 1
        grad_bf = grad.astype(BF16)
        wgrads[l] = lax.dot_general(
            acts[l],
            crop(grad_bf, radius).reshape(n_cells, channels),
            (((0,), (0,)), ((), ())),
            preferred_element_type=F32,
        )
        grad_act = lax.dot_general(
            grad_bf.reshape(-1, channels), weights[l], (((1,), (1,)), ((), ())), preferred_element_type=F32
        )
        pre = pre_acts[l]
        sigma = jax.nn.sigmoid(pre)
        grad_pre = inside(
            (grad_act.reshape(pre.shape) * (sigma * (1.0 + pre * (1.0 - sigma)))).astype(BF16), radius
        )
        field = crop(fields[l], 0)
        own = crop(grad_pre, radius).astype(F32)
        taps = []
        for a in range(3):
            for b in range(3):
                taps.append(
                    jnp.sum(own * field[a : a + lat_rows, b : b + lon_cols].astype(F32), axis=(0, 1))
                )
        kgrads[l] = jnp.stack(taps)
        grad = crop(grad, 1) + depthwise(grad_pre, kernels[l], 2, -1)
    cell_grad = (grad.reshape(n_cells, channels) / divisor).astype(BF16)
    slot_grad = lax.dot_general(
        onehot, cell_grad, (((0,), (0,)), ((), ())), preferred_element_type=F32
    ).astype(BF16)
    returned = lax.all_to_all(
        slot_grad.reshape(spatial, 1, cap, channels),
        ("lon", "lat"),
        split_axis=0,
        concat_axis=1,
        tiled=True,
    )
    weight_grad, kernel_grad = reduce_params(jnp.stack(wgrads), jnp.stack(kgrads))
    obs_grad = jnp.dot(
        place, returned.reshape(spatial * cap, channels), preferred_element_type=F32
    ).astype(BF16)
    return (state[None], weight_grad, kernel_grad, obs_grad[None])


def solution(mesh):
    placed = (
        P("ens", ("lon", "lat"), None),
        P("ens", ("lon", "lat"), None),
        P("ens", ("lon", "lat")),
        P("ens", "lat", "lon", None),
        P("ens", "lat", "lon", None),
        P(),
        P(),
    )
    return jax.shard_map(
        on_device,
        mesh=mesh,
        in_specs=placed,
        out_specs=(P("ens", "lat", "lon", None), P(), P(), P("ens", ("lon", "lat"), None)),
        check_vma=False,
    )
```

time: 781 us -> 185 us (0.24)
  waiting for transfers between devices: 465 us -> 35.3 us
  blocking collectives: 127 us -> 0 us
  starting transfers between devices: 150 us -> 59.9 us
  Pallas kernels: 0 us -> 55.4 us
  between operations: 14.8 us -> 1.26 us
  other arithmetic: 5.11 us -> 13.9 us
    psum x1 -> x0, waiting for transfers between devices: 369 us -> none  [on_device(): lax.psum((weight_grad, kernel_grad), ('lon', 'lat', 'ens'))]
    psum x1 -> x0, blocking collectives: 127 us -> none  [on_device(): lax.psum((weight_grad, kernel_grad), ('lon', 'lat', 'ens'))]
    pallas_call x0 -> x1, Pallas kernels: none -> 55.4 us  [reduce_params(): pl.pallas_call(reduce_kernel, out_shape=(jax.ShapeDtypeStruct((rows, chan...]
    ppermute x16 -> x4, starting transfers between devices: 75.9 us -> 21 us  [with_halo(): lax.ppermute(lax.slice_in_dim(block, 0, width, axis=dim), axis, backward)]
    ppermute x16 -> x4, starting transfers between devices: 41.1 us -> 12 us  [with_halo(): lax.ppermute(lax.slice_in_dim(block, block.shape[dim] - width, None, axis...]
    ppermute x16 -> x4, waiting for transfers between devices: 40.1 us -> 11.1 us  [with_halo(): lax.ppermute(lax.slice_in_dim(block, block.shape[dim] - width, None, axis...]
    ppermute x16 -> x4, waiting for transfers between devices: 28.8 us -> 0.01 us  [with_halo(): lax.ppermute(lax.slice_in_dim(block, 0, width, axis=dim), axis, backward)]
    all_to_all x3 -> x2, starting transfers between devices: 32.7 us -> 26.9 us  [the longest x1 20.5 us: on_device(): lax.all_to_all(packed[None], ('lon', 'lat'), split_axis=1, concat_axis=0,...]
  transfers between devices with their start and end apart: 36 -> 10, of which waited for: 19 -> 2; matrix products, arithmetic and copies ran while one was open for 1% -> 6% of each run, Pallas kernels for 0% -> 30%
where the time goes in v1:
time: 185 us
  starting transfers between devices  59.9 us (32%)
  Pallas kernels  55.4 us (30%)
  waiting for transfers between devices  35.3 us (19%)
  other arithmetic  13.9 us (8%)
  matrix products  12.2 us (7%)
  local copies, waits for them, and re-layouts  6.52 us (4%)
    pallas_call x1, Pallas kernels, reduce_params(): pl.pallas_call(reduce_kernel, out_shape=(jax.ShapeDtypeStruct((rows, chan...  55.4 us
    all_to_all x1, waiting for transfers between devices, on_device(): lax.all_to_all(packed[None], ('lon', 'lat'), split_axis=1, concat_axis=0,...  24.2 us
    ppermute x4, starting transfers between devices, with_halo(): lax.ppermute(lax.slice_in_dim(block, 0, width, axis=dim), axis, backward)  21 us
    all_to_all x1, starting transfers between devices, on_device(): lax.all_to_all(packed[None], ('lon', 'lat'), split_axis=1, concat_axis=0,...  20.5 us
    ppermute x4, starting transfers between devices, with_halo(): lax.ppermute(lax.slice_in_dim(block, block.shape[dim] - width, None, axis...  12 us
    ppermute x4, waiting for transfers between devices, with_halo(): lax.ppermute(lax.slice_in_dim(block, block.shape[dim] - width, None, axis...  11.1 us
    all_to_all x1, starting transfers between devices, on_device(): lax.all_to_all(slot_grad.reshape(spatial, 1, cap, channels), ('lon', 'lat...  6.39 us
    dot_general x4, matrix products, on_device(): lax.dot_general(acts[l], crop(grad_bf, radius).reshape(n_cells, channels)...  4.18 us
  transfers between devices with their start and end apart: 10, of which 2 were waited for; matrix products, arithmetic and copies ran while one was open for 6% of the time, Pallas kernels for 30%

profile of v1, /device:TPU:1, one launch (start us, length us, event | category | flops | bytes accessed | tf_op | source)
XLA Modules:
  0.0 184.5 jit_solution(13843098711511980000)
XLA Ops:
  0.6 1.0 fusion.20
  1.6 0.7 multiply_add_fusion.1
  2.3 0.7 broadcast_add_fusion
  3.0 0.9 fusion.21
  4.1 0.4 convolution_convert_fusion.1
  4.6 1.1 maximum_bitcast_fusion
  5.7 20.5 %all-to-all-start = ((bf16[1,128,5,256]{3,2,0,1:T(8,128)(2,1)}), bf16[1,128,5,256]{3,2,0,1:T(8,128)(2,1)S(1)}, u32[]{:S(2)}, u32[]{:S(2)}) async-start(bf16[1,128,5,256]{3,2,0,1:T(8,128)(2,1)} %maximum_bitcast_fusion), calls=%async_computation | async-start | bytes 1048576 | tf_op jit(solution)/shard_map/all_to_all | solution.py:273
  26.2 1.3 collective-permute-start.5
  27.5 4.0 %collective-permute-start.4 = (bf16[4,32,256]{2,1,0:T(8,128)(2,1)S(1)}, bf16[4,32,256]{2,1,0:T(8,128)(2,1)S(1)}, u32[]{:S(2)}, u32[]{:S(2)}) collective-permute-start(bf16[4,32,256]{2,1,0:T(8,128)(2,1)S(1)} %get-tuple-element.84), channel_id=1, source_target_pairs={{0,4},{4,8},{8,12},{1,5},{5,9},{9,13},{2,6},{6,10},{10,14},{3,7},{... | collective-permute-start | bytes 196616 | tf_op jit(solution)/shard_map/ppermute | solution.py:203
  31.7 24.2 %all-to-all-done = bf16[1,128,5,256]{3,2,0,1:T(8,128)(2,1)S(1)} async-done(((bf16[1,128,5,256]{3,2,0,1:T(8,128)(2,1)}), bf16[1,128,5,256]{3,2,0,1:T(8,128)(2,1)S(1)}, u32[]{:S(2)}, u32[]{:S(2)}) %all-to-all-start) | async-done | bytes 327712 | tf_op jit(solution)/shard_map/all_to_all | solution.py:273
  56.8 1.3 collective-permute-start.1
  58.1 4.0 %collective-permute-start = (bf16[8,32,256]{2,1,0:T(8,128)(2,1)S(1)}, bf16[8,32,256]{2,1,0:T(8,128)(2,1)S(1)}, u32[]{:S(2)}, u32[]{:S(2)}) collective-permute-start(bf16[8,32,256]{2,1,0:T(8,128)(2,1)S(1)} %bitcast.156), channel_id=1, source_target_pairs={{0,4},{4,8},{8,12},{1,5},{5,9},{9,13},{2,6},{6,10},{10,14},{3,7},{... | collective-permute-start | bytes 393224 | tf_op jit(solution)/shard_map/ppermute | solution.py:203
  62.2 6.4 %collective-permute-start.7 = (bf16[16,4,256]{2,1,0:T(4,128)(2,1)S(1)}, bf16[16,4,256]{2,1,0:T(4,128)(2,1)S(1)}, u32[]{:S(2)}, u32[]{:S(2)}) collective-permute-start(bf16[16,4,256]{2,1,0:T(4,128)(2,1)S(1)} %get-tuple-element.82), channel_id=1, source_target_pairs={{16,0},{32,16},{48,32},{64,48},{80,64},{96,80},{112,96},{128,112},... | collective-permute-start | bytes 98312 | tf_op jit(solution)/shard_map/ppermute | solution.py:206
  68.6 1.9 %collective-permute-start.6 = (bf16[16,4,256]{2,1,0:T(4,128)(2,1)S(1)}, bf16[16,4,256]{2,1,0:T(4,128)(2,1)S(1)}, u32[]{:S(2)}, u32[]{:S(2)}) collective-permute-start(bf16[16,4,256]{2,1,0:T(4,128)(2,1)S(1)} %get-tuple-element.81), channel_id=1, source_target_pairs={{0,16},{16,32},{32,48},{48,64},{64,80},{80,96},{96,112},{112,128},... | collective-permute-start | bytes 98312 | tf_op jit(solution)/shard_map/ppermute | solution.py:203
  70.5 12.1 %collective-permute-start.3 = (bf16[24,8,256]{2,1,0:T(8,128)(2,1)S(1)}, bf16[24,8,256]{2,1,0:T(8,128)(2,1)S(1)}, u32[]{:S(2)}, u32[]{:S(2)}) collective-permute-start(bf16[24,8,256]{2,1,0:T(8,128)(2,1)S(1)} %get-tuple-element.78), channel_id=1, source_target_pairs={{16,0},{32,16},{48,32},{64,48},{80,64},{96,80},{112,96},{128,112},... | collective-permute-start | bytes 294920 | tf_op jit(solution)/shard_map/ppermute | solution.py:206
  82.6 2.1 %collective-permute-start.2 = (bf16[24,8,256]{2,1,0:T(8,128)(2,1)S(1)}, bf16[24,8,256]{2,1,0:T(8,128)(2,1)S(1)}, u32[]{:S(2)}, u32[]{:S(2)}) collective-permute-start(bf16[24,8,256]{2,1,0:T(8,128)(2,1)S(1)} %get-tuple-element.77), channel_id=1, source_target_pairs={{0,16},{16,32},{32,48},{48,64},{64,80},{80,96},{96,112},{112,128},... | collective-permute-start | bytes 294920 | tf_op jit(solution)/shard_map/ppermute | solution.py:203
  84.8 0.9 convert_multiply_fusion.40
  85.6 11.1 %collective-permute-done.2 = bf16[24,8,256]{2,1,0:T(8,128)(2,1)S(1)} collective-permute-done((bf16[24,8,256]{2,1,0:T(8,128)(2,1)S(1)}, bf16[24,8,256]{2,1,0:T(8,128)(2,1)S(1)}, u32[]{:S(2)}, u32[]{:S(2)}) %collective-permute-start.2) | collective-permute-done | bytes 98336 | tf_op jit(solution)/shard_map/ppermute | solution.py:203
  96.8 1.1 multiply_convert_fusion
  97.8 0.3 fusion.3
  98.2 1.0 multiply_convert_fusion.1
  99.5 0.9 multiply_convert_fusion.2
  100.7 0.6 add_divide_fusion
  101.3 0.5 fusion.9
  101.8 0.9 fusion.63
  102.6 0.6 fusion.121
  103.2 0.9 convolution_bitcast_fusion.1
  104.1 0.4 fusion.11
  104.5 0.9 fusion.54
  105.4 0.5 fusion.120
  105.9 0.9 convolution_bitcast_fusion.2
  107.1 0.9 fusion.45
  108.0 0.4 fusion.119
  108.7 0.4 copy-done.5
  109.5 0.3 convolution_convert_fusion
  109.9 0.8 reshape.293
  110.7 6.4 %all-to-all-start.1 = ((bf16[128,1,4,256]{3,2,1,0:T(4,128)(2,1)}), bf16[128,1,4,256]{3,2,1,0:T(4,128)(2,1)S(1)}, u32[]{:S(2)}, u32[]{:S(2)}) async-start(bf16[128,1,4,256]{3,2,1,0:T(4,128)(2,1)} %bitcast.107), calls=%async_computation.1 | async-start | bytes 524288 | tf_op jit(solution)/shard_map/all_to_all | solution.py:341
  117.2 0.7 stack.186
  117.9 1.4 stack.175
  119.7 0.6 select_maximum_fusion.k_ref
  120.3 1.1 convolution_bitcast_fusion.3
  121.5 1.2 convolution_bitcast_fusion
  122.8 1.0 pad_maximum_fusion
  123.8 55.4 %param_sum.1 = (f32[1024,256]{1,0:T(8,128)}, f32[4,16,256]{2,1,0:T(8,128)}) custom-call(f32[1024,256]{1,0:T(8,128)} %bitcast.154, f32[4,16,256]{2,1,0:T(8,128)} %select_maximum_fusion.k_ref), custom_call_target="tpu_custom_call" | custom-call | tf_op jit(solution)/shard_map/param_sum/pallas_call | solution.py:168
  179.2 1.6 copy.22
  180.8 1.7 fusion.18
  182.6 0.9 fusion.17
  183.5 1.0 copy.24
  (72 shorter events, 3.5 us)
Async XLA Ops:
  0.6 3.4 %copy-start = (bf16[1,256,256]{2,1,0:T(8,128)(2,1)S(1)}, bf16[1,256,256]{2,1,0:T(8,128)(2,1)}, u32[]{:S(2)}) copy-start(bf16[1,256,256]{2,1,0:T(8,128)(2,1)} %param.7) | copy-start | bytes 393220
  4.6 21.6 %copy-start.1 = (bf16[1,8,32,256]{3,2,1,0:T(8,128)(2,1)S(1)}, bf16[1,8,32,256]{3,2,1,0:T(8,128)(2,1)}, u32[]{:S(2)}) copy-start(bf16[1,8,32,256]{3,2,1,0:T(8,128)(2,1)} %param.11) | copy-start | bytes 393220
  4.6 27.0 %copy-start.6 = (f32[4,9,256]{2,0,1:T(4,128)S(1)}, f32[4,9,256]{2,0,1:T(4,128)}, u32[]{:S(2)}) copy-start(f32[4,9,256]{2,0,1:T(4,128)} %param.12) | copy-start | bytes 110596
  5.7 50.9 %copy-start.14 = (bf16[1,8,32,256]{3,2,1,0:T(8,128)(2,1)S(1)}, bf16[1,8,32,256]{3,2,1,0:T(8,128)(2,1)}, u32[]{:S(2)}) copy-start(bf16[1,8,32,256]{3,2,1,0:T(8,128)(2,1)} %param.10) | copy-start | bytes 393220
  5.7 50.2 %all-to-all-start = ((bf16[1,128,5,256]{3,2,0,1:T(8,128)(2,1)}), bf16[1,128,5,256]{3,2,0,1:T(8,128)(2,1)S(1)}, u32[]{:S(2)}, u32[]{:S(2)}) async-start(bf16[1,128,5,256]{3,2,0,1:T(8,128)(2,1)} %maximum_bitcast_fusion), calls=%async_computation | async-start | bytes 1048576 | tf_op jit(solution)/shard_map/all_to_all | solution.py:273
  26.2 35.9 %collective-permute-start.5 = (bf16[4,32,256]{2,1,0:T(8,128)(2,1)S(1)}, bf16[4,32,256]{2,1,0:T(8,128)(2,1)S(1)}, u32[]{:S(2)}, u32[]{:S(2)}) collective-permute-start(bf16[4,32,256]{2,1,0:T(8,128)(2,1)S(1)} %get-tuple-element.85), channel_id=1, source_target_pairs={{4,0},{8,4},{12,8},{5,1},{9,5},{13,9},{6,2},{10,6},{14,10},{7,3},{... | collective-permute-start | bytes 196616 | tf_op jit(solution)/shard_map/ppermute | solution.py:206
  27.5 34.6 %collective-permute-start.4 = (bf16[4,32,256]{2,1,0:T(8,128)(2,1)S(1)}, bf16[4,32,256]{2,1,0:T(8,128)(2,1)S(1)}, u32[]{:S(2)}, u32[]{:S(2)}) collective-permute-start(bf16[4,32,256]{2,1,0:T(8,128)(2,1)S(1)} %get-tuple-element.84), channel_id=1, source_target_pairs={{0,4},{4,8},{8,12},{1,5},{5,9},{9,13},{2,6},{6,10},{10,14},{3,7},{... | collective-permute-start | bytes 196616 | tf_op jit(solution)/shard_map/ppermute | solution.py:203
  56.8 13.7 %collective-permute-start.1 = (bf16[8,32,256]{2,1,0:T(8,128)(2,1)S(1)}, bf16[8,32,256]{2,1,0:T(8,128)(2,1)S(1)}, u32[]{:S(2)}, u32[]{:S(2)}) collective-permute-start(bf16[8,32,256]{2,1,0:T(8,128)(2,1)S(1)} %bitcast.155), channel_id=1, source_target_pairs={{4,0},{8,4},{12,8},{5,1},{9,5},{13,9},{6,2},{10,6},{14,10},{7,3},{... | collective-permute-start | bytes 393224 | tf_op jit(solution)/shard_map/ppermute | solution.py:206
  58.1 12.4 %collective-permute-start = (bf16[8,32,256]{2,1,0:T(8,128)(2,1)S(1)}, bf16[8,32,256]{2,1,0:T(8,128)(2,1)S(1)}, u32[]{:S(2)}, u32[]{:S(2)}) collective-permute-start(bf16[8,32,256]{2,1,0:T(8,128)(2,1)S(1)} %bitcast.156), channel_id=1, source_target_pairs={{0,4},{4,8},{8,12},{1,5},{5,9},{9,13},{2,6},{6,10},{10,14},{3,7},{... | collective-permute-start | bytes 393224 | tf_op jit(solution)/shard_map/ppermute | solution.py:203
  62.2 22.6 %collective-permute-start.7 = (bf16[16,4,256]{2,1,0:T(4,128)(2,1)S(1)}, bf16[16,4,256]{2,1,0:T(4,128)(2,1)S(1)}, u32[]{:S(2)}, u32[]{:S(2)}) collective-permute-start(bf16[16,4,256]{2,1,0:T(4,128)(2,1)S(1)} %get-tuple-element.82), channel_id=1, source_target_pairs={{16,0},{32,16},{48,32},{64,48},{80,64},{96,80},{112,96},{128,112},... | collective-permute-start | bytes 98312 | tf_op jit(solution)/shard_map/ppermute | solution.py:206
  68.6 16.2 %collective-permute-start.6 = (bf16[16,4,256]{2,1,0:T(4,128)(2,1)S(1)}, bf16[16,4,256]{2,1,0:T(4,128)(2,1)S(1)}, u32[]{:S(2)}, u32[]{:S(2)}) collective-permute-start(bf16[16,4,256]{2,1,0:T(4,128)(2,1)S(1)} %get-tuple-element.81), channel_id=1, source_target_pairs={{0,16},{16,32},{32,48},{48,64},{64,80},{80,96},{96,112},{112,128},... | collective-permute-start | bytes 98312 | tf_op jit(solution)/shard_map/ppermute | solution.py:203
  70.5 15.1 %collective-permute-start.3 = (bf16[24,8,256]{2,1,0:T(8,128)(2,1)S(1)}, bf16[24,8,256]{2,1,0:T(8,128)(2,1)S(1)}, u32[]{:S(2)}, u32[]{:S(2)}) collective-permute-start(bf16[24,8,256]{2,1,0:T(8,128)(2,1)S(1)} %get-tuple-element.78), channel_id=1, source_target_pairs={{16,0},{32,16},{48,32},{64,48},{80,64},{96,80},{112,96},{128,112},... | collective-permute-start | bytes 294920 | tf_op jit(solution)/shard_map/ppermute | solution.py:206
  82.6 14.1 %collective-permute-start.2 = (bf16[24,8,256]{2,1,0:T(8,128)(2,1)S(1)}, bf16[24,8,256]{2,1,0:T(8,128)(2,1)S(1)}, u32[]{:S(2)}, u32[]{:S(2)}) collective-permute-start(bf16[24,8,256]{2,1,0:T(8,128)(2,1)S(1)} %get-tuple-element.77), channel_id=1, source_target_pairs={{0,16},{16,32},{32,48},{48,64},{64,80},{80,96},{96,112},{112,128},... | collective-permute-start | bytes 294920 | tf_op jit(solution)/shard_map/ppermute | solution.py:203
  96.7 1.1 copy-start.13
  108.4 0.7 copy-start.5
  109.4 7.7 %copy-start.7 = (f32[256]{0:T(256)S(1)}, f32[256]{0:T(256)}, u32[]{:S(2)}) copy-start(f32[256]{0:T(256)} %get-tuple-element.52) | copy-start | bytes 3076
  109.4 7.7 %copy-start.8 = (f32[256]{0:T(256)S(1)}, f32[256]{0:T(256)}, u32[]{:S(2)}) copy-start(f32[256]{0:T(256)} %get-tuple-element.53) | copy-start | bytes 3076
  109.4 7.7 %copy-start.9 = (f32[256]{0:T(256)S(1)}, f32[256]{0:T(256)}, u32[]{:S(2)}) copy-start(f32[256]{0:T(256)} %get-tuple-element.54) | copy-start | bytes 3076
  109.4 7.8 %copy-start.10 = (f32[256]{0:T(256)S(1)}, f32[256]{0:T(256)}, u32[]{:S(2)}) copy-start(f32[256]{0:T(256)} %get-tuple-element.37) | copy-start | bytes 3076
  109.4 7.7 %copy-start.11 = (f32[256]{0:T(256)S(1)}, f32[256]{0:T(256)}, u32[]{:S(2)}) copy-start(f32[256]{0:T(256)} %get-tuple-element.38) | copy-start | bytes 3076
  109.5 7.6 %copy-start.12 = (f32[256]{0:T(256)S(1)}, f32[256]{0:T(256)}, u32[]{:S(2)}) copy-start(f32[256]{0:T(256)} %get-tuple-element.39) | copy-start | bytes 3076
  110.7 71.8 %all-to-all-start.1 = ((bf16[128,1,4,256]{3,2,1,0:T(4,128)(2,1)}), bf16[128,1,4,256]{3,2,1,0:T(4,128)(2,1)S(1)}, u32[]{:S(2)}, u32[]{:S(2)}) async-start(bf16[128,1,4,256]{3,2,1,0:T(4,128)(2,1)} %bitcast.107), calls=%async_computation.1 | async-start | bytes 524288 | tf_op jit(solution)/shard_map/all_to_all | solution.py:341
  121.5 1.3 copy-start.3
  121.5 1.3 copy-start.4
  179.2 4.3 %copy-start.2 = (f32[1024,256]{1,0:T(8,128)S(1)}, f32[1024,256]{1,0:T(8,128)}, u32[]{:S(2)}) copy-start(f32[1024,256]{1,0:T(8,128)} %get-tuple-element.6) | copy-start | bytes 3145732

commit v2 on v1

--- a/solution.py
+++ b/solution.py
@@ -193,22 +193,178 @@
     return w.reshape(wgrad.shape), k[:, :taps]
 
 
-def with_halo(block, sides, width):
-    for axis, dim, periodic in sides:
-        count = lax.axis_size(axis)
-        forward = [(i, i + 1) for i in range(count - 1)]
-        if periodic:
-            forward.append((count - 1, 0))
-        backward = [(target, source) for source, target in forward]
-        low = lax.ppermute(
-            lax.slice_in_dim(block, block.shape[dim] - width, None, axis=dim), axis, forward
+def route_kernel(
+    send_ref, base_ref, seed_ref, wide_ref, seed_out, cells_ref,
+    r1, perm, z_send, r2, tile, strip, seed_strip, h_row, h_col, s_row, s_mid, s_end,
+    p_ss, p_rs, z_ss, z_rs, h_ss, h_rs, s_ss, s_rs,
+):
+    lon = lax.axis_index("lon")
+    x = lax.axis_index("lat")
+    ens = lax.axis_index("ens")
+    n_lon = lax.axis_size("lon")
+    zl, y = lon // NY, lon % NY
+    mine = y * NX + x
+
+    def at(plon, px):
+        return {"lon": plon, "lat": px, "ens": ens}
+
+    plane = []
+    for k in range(1, NX * NY):
+        px, py = (x + k % NX) % NX, (y + k // NX) % NY
+        plane.append((py * NX + px, at(zl * NY + py, px), k))
+    along = []
+    for k in range(1, NZL):
+        pz = (zl + k) % NZL
+        along.append((pz, at(pz * NY + y, x), k))
+    west, east = (lon + n_lon - 1) % n_lon, (lon + 1) % n_lon
+    north, south = (x + NX - 1) % NX, (x + 1) % NX
+    lats = (south, x, north)
+
+    barrier = pltpu.get_barrier_semaphore()
+    greeted = [p for _, p, _ in plane] + [p for _, p, _ in along]
+    greeted += [at(lon, north), at(lon, south)] + [at(w, q) for w in (west, east) for q in lats]
+    for peer in greeted:
+        pl.semaphore_signal(barrier, inc=1, device_id=peer, device_id_type=MESH)
+    rows, cols, channels = base_ref.shape
+    seed = seed_ref[...].astype(F32)
+    seed_strip[0] = seed[:, :8].reshape(rows * 8, channels).astype(BF16)
+    seed_strip[1] = seed[:, cols - 8 :].reshape(rows * 8, channels).astype(BF16)
+    pl.semaphore_wait(barrier, len(greeted))
+
+    def copy(src, dst, ss, rs, peer):
+        return pltpu.make_async_remote_copy(
+            src_ref=src, dst_ref=dst, send_sem=ss, recv_sem=rs, device_id=peer, device_id_type=MESH
         )
-        high = lax.ppermute(lax.slice_in_dim(block, 0, width, axis=dim), axis, backward)
-        block = jnp.concatenate([low, block, high], axis=dim)
-    return block
-
-
-SIDES = (("lat", 0, False), ("lon", 1, True))
+
+    def go(copies):
+        for c in copies:
+            c.start()
+        return copies
+
+    def done(copies):
+        for c in copies:
+            c.wait()
+
+    live = go([copy(send_ref.at[d], r1.at[mine], p_ss.at[k], p_rs.at[k], peer) for d, peer, k in plane])
+    edge = s_row.shape[1]
+    cut = edge * 8
+    seeds = [
+        copy(seed_ref.at[rows - edge : rows], s_row.at[0], s_ss.at[0], s_rs.at[0], at(lon, south)),
+        copy(seed_ref.at[0:edge], s_row.at[1], s_ss.at[1], s_rs.at[1], at(lon, north)),
+    ]
+    for side, other in ((0, east), (1, west)):
+        src = seed_strip.at[1 - side]
+        n = 2 + 3 * side
+        seeds += [
+            copy(src.at[rows * 8 - cut : rows * 8], s_end.at[side, 0], s_ss.at[n], s_rs.at[n], at(other, south)),
+            copy(src, s_mid.at[side], s_ss.at[n + 1], s_rs.at[n + 1], at(other, x)),
+            copy(src.at[0:cut], s_end.at[side, 1], s_ss.at[n + 2], s_rs.at[n + 2], at(other, north)),
+        ]
+    go(seeds)
+    r1[mine] = send_ref[mine]
+    total = perm.shape[0]
+    items = total // (NX * NY * NZL)
+    i = lax.broadcasted_iota(jnp.int32, (total, 1), 0)
+    pz = i // (items * NX * NY)
+    rest = i - pz * (items * NX * NY)
+    source = (rest % (NX * NY)) * (items * NZL) + (rest // (NX * NY)) * NZL + pz
+    j = lax.broadcasted_iota(jnp.int32, (total, total), 1)
+    perm[...] = jnp.where(j == source, 1.0, 0.0).astype(BF16)
+    done(live)
+    flat = r1[...].astype(F32).reshape(total, channels).astype(BF16)
+    z_send[...] = (
+        jnp.dot(perm[...], flat, preferred_element_type=F32).astype(BF16).reshape(z_send.shape)
+    )
+    live = go([copy(z_send.at[p], r2.at[zl], z_ss.at[k], z_rs.at[k], peer) for p, peer, k in along])
+    r2[zl] = z_send[zl]
+    done(live)
+    group = NX * NY
+    spatial = group * NZL
+    n_cells = rows * cols
+    cells = r2[:, (items - 1) * group : items * group].reshape(spatial, channels)
+    cells_ref[...] = cells
+    cells = cells.astype(F32)
+    lane = lax.broadcasted_iota(jnp.int32, (spatial, n_cells), 1).astype(F32)
+    ones = jnp.ones((spatial, channels), BF16)
+    summed = jnp.zeros((n_cells, channels), F32)
+    counts = jnp.zeros((n_cells, channels), F32)
+    for p in range(items - 1):
+        hot = jnp.where(cells[:, p : p + 1] == lane, 1.0, 0.0).astype(BF16)
+        vals = r2[:, p * group : (p + 1) * group].reshape(spatial, channels)
+        turn = (((0,), (0,)), ((), ()))
+        summed = summed + lax.dot_general(hot, vals, turn, preferred_element_type=F32)
+        counts = counts + lax.dot_general(hot, ones, turn, preferred_element_type=F32)
+    base = base_ref[...].astype(F32).reshape(n_cells, channels)
+    h0 = (base + summed / jnp.maximum(counts, 1.0)).reshape(rows, cols, channels)
+    tile[...] = h0.astype(BF16)
+    strip[0] = h0[:, :8].reshape(rows * 8, channels).astype(BF16)
+    strip[1] = h0[:, cols - 8 :].reshape(rows * 8, channels).astype(BF16)
+    halos = []
+    for side, other in ((0, east), (1, west)):
+        for t, q in enumerate(lats):
+            n = 2 + 3 * side + t
+            halos.append(copy(strip.at[1 - side], h_col.at[side, t], h_ss.at[n], h_rs.at[n], at(other, q)))
+    halos += [
+        copy(tile, h_row.at[0], h_ss.at[0], h_rs.at[0], at(lon, south)),
+        copy(tile, h_row.at[1], h_ss.at[1], h_rs.at[1], at(lon, north)),
+    ]
+    go(halos)
+    done(seeds)
+
+    def put(out, row, left, mid, right, keep):
+        line = jnp.concatenate([left.astype(F32), mid.astype(F32), right.astype(F32)], axis=0)
+        if keep is not None:
+            line = jnp.where(keep, line, 0.0)
+        out[row] = line.astype(BF16)
+
+    has_north, has_south = x > 0, x < NX - 1
+    for r in range(edge):
+        c = r * 8
+        put(seed_out, r, s_end[0, 0].astype(F32)[c : c + 8], s_row[0, r], s_end[1, 0].astype(F32)[c : c + 8], has_north)
+        put(
+            seed_out, edge + rows + r,
+            s_end[0, 1].astype(F32)[c : c + 8], s_row[1, r], s_end[1, 1].astype(F32)[c : c + 8], has_south,
+        )
+    for r in range(rows):
+        c = r * 8
+        put(seed_out, edge + r, s_mid[0].astype(F32)[c : c + 8], seed[r], s_mid[1].astype(F32)[c : c + 8], None)
+    done(halos)
+    left = [h_col[0, t].astype(F32) for t in range(3)]
+    right = [h_col[1, t].astype(F32) for t in range(3)]
+    for r in range(rows):
+        c = r * 8
+        put(wide_ref, r, left[0][c : c + 8], h_row[0, r], right[0][c : c + 8], has_north)
+        put(wide_ref, rows + r, left[1][c : c + 8], tile[r], right[1][c : c + 8], None)
+        put(wide_ref, 2 * rows + r, left[2][c : c + 8], h_row[1, r], right[2][c : c + 8], has_south)
+
+
+def route(send, base, seed, edge):
+    rows, cols, channels = base.shape
+    spatial = NX * NY * NZL
+    items = send.shape[1] // NZL
+    V = pltpu.VMEM
+    D = pltpu.SemaphoreType.DMA
+    return pl.pallas_call(
+        route_kernel,
+        out_shape=(
+            jax.ShapeDtypeStruct((3 * rows, cols + 16, channels), BF16),
+            jax.ShapeDtypeStruct((2 * edge + rows, cols + 16, channels), BF16),
+            jax.ShapeDtypeStruct((spatial, channels), BF16),
+        ),
+        in_specs=[pl.BlockSpec(memory_space=V)] * 3,
+        out_specs=(pl.BlockSpec(memory_space=V),) * 3,
+        scratch_shapes=[
+            V(send.shape, BF16), V((items * spatial, items * spatial), BF16),
+            V((NZL, items * NX * NY, channels), BF16), V((NZL, items * NX * NY, channels), BF16),
+            V(base.shape, BF16), V((2, rows * 8, channels), BF16), V((2, rows * 8, channels), BF16),
+            V((2, rows, cols, channels), BF16), V((2, 3, rows * 8, channels), BF16),
+            V((2, edge, cols, channels), BF16), V((2, rows * 8, channels), BF16),
+            V((2, 2, edge * 8, channels), BF16),
+            D((NX * NY,)), D((NX * NY,)), D((NZL,)), D((NZL,)), D((8,)), D((8,)), D((8,)), D((8,)),
+        ],
+        compiler_params=pltpu.CompilerParams(collective_id=1, has_side_effects=True),
+        name="route",
+    )(send, base, seed)
 
 
 def depthwise(padded, kernel_rows, offset, sign):
@@ -248,8 +404,6 @@
         row = lax.broadcasted_iota(jnp.int32, (v.shape[0], 1, 1), 0)
         row = row + lax.axis_index("lat") * lat_rows - radius
         return jnp.where((row >= 0) & (row < n_lat * lat_rows), v, jnp.zeros((), v.dtype))
-
-    seed_wide = with_halo(seed_grad[0], tuple(SIDES), n_layers)
 
     target = obs_tile[0, :, 0]
     matches = (target[:, None] == jnp.arange(spatial, dtype=jnp.int32)[None, :]).astype(BF16)
@@ -270,23 +424,16 @@
     packed = jnp.concatenate(
         [send_values.reshape(spatial, cap, channels), send_cells.reshape(spatial, 1, channels)], axis=1
     )
-    got = lax.all_to_all(
-        packed[None], ("lon", "lat"), split_axis=1, concat_axis=0, tiled=True
-    ).reshape(spatial, cap + 1, channels)
-    recv_values = got[:, :cap].reshape(spatial * cap, channels)
-    recv_cells = got[:, cap, :cap].astype(jnp.int32).reshape(spatial * cap)
+    send = packed.reshape(NZL, NX * NY, cap + 1, channels).transpose(1, 2, 0, 3)
+    send = send.reshape(NX * NY, (cap + 1) * NZL, channels)
+    hidden, seed_wide, cell_out = route(send, backdrop[0], seed_grad[0], n_layers)
+    seed_wide = seed_wide[:, 8 - n_layers : 8 + lon_cols + n_layers]
+    recv_cells = cell_out[:, :cap].astype(jnp.int32).reshape(spatial * cap)
     onehot_mask = recv_cells[None, :] == jnp.arange(n_cells, dtype=jnp.int32)[:, None]
     onehot = onehot_mask.astype(BF16)
-    summed = jnp.dot(onehot, recv_values, preferred_element_type=F32)
     counts = jnp.sum(onehot_mask.astype(jnp.int32), axis=1)
     divisor = jnp.maximum(counts, 1).astype(F32)[:, None]
-    hidden = (
-        (backdrop[0].reshape(n_cells, channels).astype(F32) + summed / divisor)
-        .astype(BF16)
-        .reshape(lat_rows, lon_cols, channels)
-    )
     wide = 2 * n_layers
-    hidden = with_halo(hidden, SIDES, wide)
     fields, pre_acts, acts = [], [], []
     for l in range(n_layers):
         radius = wide - 1 - l

time: 185 us -> 150 us (0.81)
  starting transfers between devices: 59.9 us -> 8.61 us
  Pallas kernels: 55.4 us -> 103 us
  waiting for transfers between devices: 35.3 us -> 0.01 us
    pallas_call x0 -> x1, Pallas kernels: none -> 46.6 us  [route(): pl.pallas_call(route_kernel, out_shape=(jax.ShapeDtypeStruct((3 * rows, c...]
    ppermute x8 -> x0, starting transfers between devices: 33 us -> none  [the longest x4 21 us: with_halo(): lax.ppermute(lax.slice_in_dim(block, 0, width, axis=dim), axis, backward)]
    all_to_all x1 -> x0, waiting for transfers between devices: 24.2 us -> none  [on_device(): lax.all_to_all(packed[None], ('lon', 'lat'), split_axis=1, concat_axis=0,...]
    all_to_all x1 -> x0, starting transfers between devices: 20.5 us -> none  [on_device(): lax.all_to_all(packed[None], ('lon', 'lat'), split_axis=1, concat_axis=0,...]
    ppermute x8 -> x0, waiting for transfers between devices: 11.1 us -> none  [the longest x4 11.1 us: with_halo(): lax.ppermute(lax.slice_in_dim(block, block.shape[dim] - width, None, axis...]
    all_to_all x1, starting transfers between devices: 6.39 us -> 8.61 us  [on_device(): lax.all_to_all(slot_grad.reshape(spatial, 1, cap, channels), ('lon', 'lat...]
    another operation x4, local copies, waits for them, and re-layouts: 2.21 us -> 0.16 us  [on_device(): kgrads[l] = jnp.stack(taps)]
    dot_general x4, matrix products: 4.18 us -> 6.1 us  [on_device(): lax.dot_general(acts[l], crop(grad_bf, radius).reshape(n_cells, channels)...]
  transfers between devices with their start and end apart: 10 -> 1, of which waited for: 2 -> 0; matrix products, arithmetic and copies ran while one was open for 6% -> 9% of each run, Pallas kernels for 30% -> 38%
where the time goes in v2:
time: 150 us
  Pallas kernels  103 us (69%)
  other arithmetic  15 us (10%)
  matrix products  13.9 us (9%)
  starting transfers between devices  8.61 us (6%)
  local copies, waits for them, and re-layouts  7.82 us (5%)
    pallas_call x1, Pallas kernels, reduce_params(): pl.pallas_call(reduce_kernel, out_shape=(jax.ShapeDtypeStruct((rows, chan...  56.7 us
    pallas_call x1, Pallas kernels, route(): pl.pallas_call(route_kernel, out_shape=(jax.ShapeDtypeStruct((3 * rows, c...  46.6 us
    all_to_all x1, starting transfers between devices, on_device(): lax.all_to_all(slot_grad.reshape(spatial, 1, cap, channels), ('lon', 'lat...  8.61 us
    dot_general x4, matrix products, on_device(): lax.dot_general(acts[l], crop(grad_bf, radius).reshape(n_cells, channels)...  6.1 us
    unnamed x40, local copies, waits for them, and re-layouts  4.71 us
    convert_element_type x4, other arithmetic, on_device(): act = jax.nn.silu(pre).astype(BF16)  4.08 us
  transfers between devices with their start and end apart: 1, of which 0 were waited for; matrix products, arithmetic and copies ran while one was open for 9% of the time, Pallas kernels for 38%

profile of v2, /device:TPU:1, one launch (start us, length us, event | category | flops | bytes accessed | tf_op | source)
XLA Modules:
  0.0 149.8 jit_solution(16712603189859173987)
XLA Ops:
  0.6 1.0 fusion.18
  1.6 0.7 multiply_add_fusion.1
  2.3 0.9 fusion.121
  3.2 0.9 fusion.120
  4.2 0.7 broadcast_add_fusion
  4.9 0.9 fusion.17
  5.9 0.4 convolution_convert_fusion.1
  6.5 0.8 maximum_bitcast_fusion.send_ref
  7.3 46.6 %route.1 = (bf16[24,48,256]{2,1,0:T(8,128)(2,1)}, bf16[16,48,256]{2,1,0:T(8,128)(2,1)}, bf16[128,256]{1,0:T(8,128)(2,1)}) custom-call(bf16[16,40,256]{2,1,0:T(8,128)(2,1)} %maximum_bitcast_fusion.send_ref, bf16[8,32,256]{2,1,0:T(8,128)(2,1)} %bitcast.149, bf16[8,32,256]{2,1,0:T(8,128)(2,1)} %bitcast.150), custom_call_target="tpu_custom_call" | custom-call | tf_op jit(solution)/shard_map/route/pallas_call | solution.py:347
  54.0 1.9 %convert_multiply_fusion.40 = (f32[16,40,256]{2,1,0:T(8,128)S(1)}, bf16[16,40,256]{2,1,0:T(8,128)(2,1)}) fusion(bf16[16,48,256]{2,1,0:T(8,128)(2,1)} %get-tuple-element.10), kind=kLoop, calls=%fused_computation.95 | loop fusion | flops 491520 | bytes 1310720 | tf_op jit(solution)/shard_map/mul | solution.py:454
  56.1 1.1 multiply_convert_fusion
  57.2 0.3 fusion.3
  57.6 0.4 copy-done.4
  58.0 1.0 multiply_convert_fusion.1
  59.0 0.3 fusion.4
  59.3 0.4 copy-done.5
  59.7 0.9 multiply_convert_fusion.2
  60.6 0.3 fusion.6
  61.0 1.4 add_divide_fusion
  62.4 0.4 fusion.9
  62.8 0.4 copy-done.2
  63.3 0.6 fusion.116
  63.8 0.4 fusion.11
  64.2 0.5 fusion.115
  64.7 0.3 fusion.12
  65.1 0.4 copy-done.11
  65.4 0.4 fusion.114
  65.8 0.3 fusion.13
  66.2 0.4 copy-done.13
  66.9 0.3 convolution_convert_fusion
  67.2 0.8 reshape.270
  68.0 8.6 %all-to-all-start = ((bf16[128,1,4,256]{3,2,1,0:T(4,128)(2,1)}), bf16[128,1,4,256]{3,2,1,0:T(4,128)(2,1)S(1)}, u32[]{:S(2)}, u32[]{:S(2)}) async-start(bf16[128,1,4,256]{3,2,1,0:T(4,128)(2,1)} %bitcast.148), calls=%async_computation | async-start | bytes 524288 | tf_op jit(solution)/shard_map/all_to_all | solution.py:488
  76.6 2.0 %convolution_bitcast_fusion.1 = f32[1,256,256]{2,1,0:T(8,128)} fusion(bf16[14,38,256]{2,1,0:T(8,128)(2,1)} %copy-done.7, bf16[18,42,256]{2,1,0:T(8,128)(2,1)} %copy-done.6), kind=kOutput, calls=%fused_computation.25 | convolution fusion | flops 33554432 | bytes 524288 | tf_op jit(solution)/shard_map/dot_general | solution.py:460
  78.6 1.9 %convolution_bitcast_fusion.2 = f32[1,256,256]{2,1,0:T(8,128)} fusion(bf16[12,36,256]{2,1,0:T(8,128)(2,1)S(1)} %copy-done.12, bf16[20,44,256]{2,1,0:T(8,128)(2,1)} %copy-done.5), kind=kOutput, calls=%fused_computation.26 | convolution fusion | flops 33554432 | bytes 524288 | tf_op jit(solution)/shard_map/dot_general | solution.py:460
  80.5 0.9 fusion.60
  81.3 0.3 fusion.51
  81.7 0.3 fusion.42
  82.0 0.3 fusion.69
  82.5 0.6 select_maximum_fusion.k_ref
  83.2 1.1 convolution_bitcast_fusion.3
  84.3 1.2 fusion.76
  85.5 1.1 convolution_bitcast_fusion
  86.7 1.0 pad_maximum_fusion
  87.7 56.7 %param_sum.1 = (f32[1024,256]{1,0:T(8,128)}, f32[4,16,256]{2,1,0:T(8,128)}) custom-call(f32[1024,256]{1,0:T(8,128)} %bitcast.146, f32[4,16,256]{2,1,0:T(8,128)} %select_maximum_fusion.k_ref), custom_call_target="tpu_custom_call" | custom-call | tf_op jit(solution)/shard_map/param_sum/pallas_call | solution.py:168
  144.4 1.6 %copy.24 = f32[4,9,256]{2,0,1:T(4,128)} copy(f32[4,9,256]{2,1,0:T(8,128)} %bitcast.151) | data formatting | bytes 73728
  146.0 1.8 %fusion.16 = bf16[1,8,32,256]{3,2,1,0:T(8,128)(2,1)} fusion(bf16[8,32,256]{2,1,0:T(8,128)(2,1)S(1)} %fusion.76, bf16[18,42,256]{2,1,0:T(8,128)(2,1)S(1)} %fusion.6, bf16[4,256,256]{2,1,0:T(8,128)(2,1)} %param.13), kind=kOutput, calls=%fused_computation.33 | convolution fusion | flops 33751040 | bytes 524288 | tf_op jit(solution)/shard_map/dot_general | solution.py:448
  147.8 0.9 fusion.15
  148.8 1.0 copy.26
  (56 shorter events, 1.3 us)
Async XLA Ops:
  0.6 5.2 %copy-start = (bf16[1,256,256]{2,1,0:T(8,128)(2,1)S(1)}, bf16[1,256,256]{2,1,0:T(8,128)(2,1)}, u32[]{:S(2)}) copy-start(bf16[1,256,256]{2,1,0:T(8,128)(2,1)} %param.7) | copy-start | bytes 393220
  53.9 1.9 %copy-start.15 = (bf16[128,256]{1,0:T(8,128)(2,1)S(1)}, bf16[128,256]{1,0:T(8,128)(2,1)}, u32[]{:S(2)}) copy-start(bf16[128,256]{1,0:T(8,128)(2,1)} %get-tuple-element.13) | copy-start | bytes 196612
  53.9 2.2 %copy-start.1 = (bf16[24,48,256]{2,1,0:T(8,128)(2,1)S(1)}, bf16[24,48,256]{2,1,0:T(8,128)(2,1)}, u32[]{:S(2)}) copy-start(bf16[24,48,256]{2,1,0:T(8,128)(2,1)} %get-tuple-element.9) | copy-start | bytes 1769476
  56.1 1.1 copy-start.18
  57.2 0.8 copy-start.4
  59.0 0.8 copy-start.5
  60.6 2.2 %copy-start.6 = (bf16[18,42,256]{2,1,0:T(8,128)(2,1)}, bf16[18,42,256]{2,1,0:T(8,128)(2,1)S(1)}, u32[]{:S(2)}) copy-start(bf16[18,42,256]{2,1,0:T(8,128)(2,1)S(1)} %get-tuple-element.74) | copy-start | bytes 1161220
  60.9 1.5 copy-start.8
  62.4 0.9 copy-start.2
  63.8 0.9 copy-start.7
  64.7 0.7 copy-start.11
  65.8 0.7 copy-start.13
  68.0 79.8 %all-to-all-start = ((bf16[128,1,4,256]{3,2,1,0:T(4,128)(2,1)}), bf16[128,1,4,256]{3,2,1,0:T(4,128)(2,1)S(1)}, u32[]{:S(2)}, u32[]{:S(2)}) async-start(bf16[128,1,4,256]{3,2,1,0:T(4,128)(2,1)} %bitcast.148), calls=%async_computation | async-start | bytes 524288 | tf_op jit(solution)/shard_map/all_to_all | solution.py:488
  76.6 2.0 %copy-start.12 = (bf16[12,36,256]{2,1,0:T(8,128)(2,1)S(1)}, bf16[12,36,256]{2,1,0:T(8,128)(2,1)}, u32[]{:S(2)}) copy-start(bf16[12,36,256]{2,1,0:T(8,128)(2,1)} %copy-done.11) | copy-start | bytes 663556
  81.7 0.7 copy-start.16
  81.7 0.7 copy-start.17
  82.0 1.2 copy-start.14
  84.3 2.4 %copy-start.9 = (f32[1,256,256]{2,1,0:T(8,128)S(1)}, f32[1,256,256]{2,1,0:T(8,128)}, u32[]{:S(2)}) copy-start(f32[1,256,256]{2,1,0:T(8,128)} %convolution_bitcast_fusion.1) | copy-start | bytes 786436
  84.3 2.4 %copy-start.10 = (f32[1,256,256]{2,1,0:T(8,128)S(1)}, f32[1,256,256]{2,1,0:T(8,128)}, u32[]{:S(2)}) copy-start(f32[1,256,256]{2,1,0:T(8,128)} %convolution_bitcast_fusion.2) | copy-start | bytes 786436
  144.4 4.3 %copy-start.3 = (f32[1024,256]{1,0:T(8,128)S(1)}, f32[1024,256]{1,0:T(8,128)}, u32[]{:S(2)}) copy-start(f32[1024,256]{1,0:T(8,128)} %get-tuple-element.11) | copy-start | bytes 3145732

commit v3 on v2

--- a/solution.py
+++ b/solution.py
@@ -14,12 +14,10 @@
 
 def reduce_kernel(
     w_ref, k_ref, wo_ref, ko_ref,
-    c_send, c_recv, x_send, x_recv, y_send, y_recv, z_send, z_recv,
-    zg, yg, xg, cg,
-    kc_recv, kx_send, kx_recv, ky_send, ky_recv, kyg, kxg,
-    c_ss, c_rs, x_ss, x_rs, y_ss, y_rs, z_ss, z_rs, g_ss, g_rs,
-    kc_ss, kc_rs, kx_ss, kx_rs, ky_ss, ky_rs, kyg_ss, kyg_rs, kxg_ss, kxg_rs,
-    yg_ss, yg_rs, xg_ss, xg_rs, cg_ss, cg_rs,
+    c_send, c_recv, x_send, x_recv, z_send, z_recv, zg, out, xg, cg,
+    kc_recv, kx_send, kx_recv, kxg,
+    c_ss, c_rs, x_ss, x_rs, z_ss, z_rs, g_ss, g_rs,
+    kc_ss, kc_rs, kx_ss, kx_rs, kxg_ss, kxg_rs, xg_ss, xg_rs, cg_ss, cg_rs,
 ):
     lon = lax.axis_index("lon")
     x = lax.axis_index("lat")
@@ -27,23 +25,30 @@
     zl, y = lon // NY, lon % NY
     zh, core = ens // NC, ens % NC
     z = zh * NZL + zl
+    mine = y * NX + x
 
     def at(px, py, pz, pc):
         return {"lon": (pz % NZL) * NY + py, "lat": px, "ens": (pz // NZL) * NC + pc}
 
     other = at(x, y, z, 1 - core)
-    x_peers = [((x + k) % NX, k) for k in range(1, NX)]
-    y_peers = [((y + k) % NY, k) for k in range(1, NY)]
+    plane = []
+    for k in range(1, NX * NY):
+        px, py = (x + k % NX) % NX, (y + k // NX) % NY
+        plane.append((py * NX + px, at(px, py, z, core), k))
+    senders = []
+    for k in range(1, NX * NY):
+        px, py = (x + NX - k % NX) % NX, (y + NY - k // NX) % NY
+        senders.append((py * NX + px, k))
     z_peers = [((z + k) % NZ, k) for k in range(1, NZ)]
     g_peers = [(zh * NZL + (zl + k) % NZL, k) for k in range(1, NZL)]
 
     barrier = pltpu.get_barrier_semaphore()
-    greeted = [other]
-    greeted += [at(p, y, z, core) for p, _ in x_peers]
-    greeted += [at(x, p, z, core) for p, _ in y_peers]
-    greeted += [at(x, y, p, core) for p, _ in z_peers]
+    greeted = [other] + [p for _, p, _ in plane] + [at(x, y, p, core) for p, _ in z_peers]
     for peer in greeted:
         pl.semaphore_signal(barrier, inc=1, device_id=peer, device_id_type=MESH)
+    n, rows = c_send.shape[1], c_send.shape[2]
+    half = n * rows
+    c_send[...] = w_ref[...].astype(BF16).reshape(c_send.shape)
     pl.semaphore_wait(barrier, len(greeted))
 
     def copy(src, dst, ss, rs, peer):
@@ -60,47 +65,31 @@
         for c in copies:
             c.wait()
 
-    half = c_send.shape[1]
-    for c in range(NC):
-        c_send[c] = w_ref[c * half : (c + 1) * half].astype(BF16)
-    live = go([
-        copy(c_send.at[1 - core], c_recv, c_ss, c_rs, other),
-        copy(k_ref, kc_recv, kc_ss, kc_rs, other),
-    ])
+    order = [(d, k) for d, _, k in plane] + [(mine, 0)]
+    first = go([copy(k_ref, kc_recv, kc_ss, kc_rs, other)])
+    pieces = go([copy(c_send.at[1 - core, d], c_recv.at[d], c_ss.at[k], c_rs.at[k], other) for d, k in order])
+    done(first)
+    ksum = k_ref[...] + kc_recv[...]
+    for d in range(n):
+        r, c = (d // 2) % 2 * 8, d % 2 * 128
+        kx_send[d] = ksum[d // 4, r : r + 8, c : c + 128]
+    live = go([copy(kx_send.at[d], kx_recv.at[mine], kx_ss.at[k], kx_rs.at[k], peer) for d, peer, k in plane])
+    kx_recv[mine] = kx_send[mine]
+    for (d, k), piece in zip(order, pieces):
+        piece.wait_recv()
+        own = w_ref[pl.ds(pl.multiple_of(core * half + d * rows, rows), rows)]
+        x_send[d] = (own + c_recv[d].astype(F32)).astype(BF16)
+        if k:
+            live += go([copy(x_send.at[d], x_recv.at[mine], x_ss.at[k], x_rs.at[k], plane[k - 1][1])])
+    x_recv[mine] = x_send[mine]
+    for piece in pieces:
+        piece.wait_send()
     done(live)
-    rows = x_send.shape[1]
-    for p in range(NX):
-        mine = w_ref[pl.ds(pl.multiple_of(core * half + p * rows, rows), rows)]
-        x_send[p] = (mine + c_recv[p * rows : (p + 1) * rows].astype(F32)).astype(BF16)
-    kx_send[...] = k_ref[...] + kc_recv[...]
-    kx_recv[x] = kx_send[x]
-    live = go(
-        [copy(x_send.at[p], x_recv.at[x], x_ss.at[k], x_rs.at[k], at(p, y, z, core)) for p, k in x_peers]
-        + [copy(kx_send.at[p], kx_recv.at[x], kx_ss.at[k], kx_rs.at[k], at(p, y, z, core)) for p, k in x_peers]
-    )
-    x_recv[x] = x_send[x]
-    done(live)
-    rows = y_send.shape[1]
-    for p in range(NY):
-        part = pl.ds(p * rows, rows)
-        total = x_recv[0, part].astype(F32)
-        for q in range(1, NX):
-            total = total + x_recv[q, part].astype(F32)
-        y_send[p] = total.astype(BF16)
-    ksum = kx_recv[0] + kx_recv[1] + kx_recv[2] + kx_recv[3]
-    for p in range(NY):
-        ky_send[p] = ksum[(p // 2) * 8 : (p // 2) * 8 + 8, (p % 2) * 128 : (p % 2) * 128 + 128]
-    live = go(
-        [copy(y_send.at[p], y_recv.at[y], y_ss.at[k], y_rs.at[k], at(x, p, z, core)) for p, k in y_peers]
-        + [copy(ky_send.at[p], ky_recv.at[y], ky_ss.at[k], ky_rs.at[k], at(x, p, z, core)) for p, k in y_peers]
-    )
-    y_recv[y] = y_send[y]
-    ky_recv[y] = ky_send[y]
-    done(live)
-    total = y_recv[0].astype(F32)
-    for q in range(1, NY):
-        total = total + y_recv[q].astype(F32)
-    ktile = ky_recv[0] + ky_recv[1] + ky_recv[2] + ky_recv[3]
+    total = x_recv[0].astype(F32)
+    ktile = kx_recv[0]
+    for q in range(1, n):
+        total = total + x_recv[q].astype(F32)
+        ktile = ktile + kx_recv[q]
     for p in range(NZL):
         z_send[p, 0] = total[(p // 2) * 8 : (p // 2) * 8 + 8, (p % 2) * 128 : (p % 2) * 128 + 128]
         z_send[p, 1] = ktile
@@ -113,48 +102,31 @@
     for q in range(1, NZ):
         both = both + z_recv[q]
     zg[zl] = both[0]
-    kyg[y] = both[1]
+    kxg[mine] = both[1]
     live = go([copy(zg.at[zl], zg.at[zl], g_ss.at[k], g_rs.at[k], at(x, y, p, core)) for p, k in g_peers])
-    klive = go([
-        copy(kyg.at[y], kyg.at[y], kyg_ss.at[k], kyg_rs.at[k], at(x, p, z, core)) for p, k in y_peers
-    ])
-    done(klive)
-    kxg[x] = kyg[...]
-    klive = go([
-        copy(kyg, kxg.at[x], kxg_ss.at[k], kxg_rs.at[k], at(p, y, z, core)) for p, k in x_peers
-    ])
+    klive = go([copy(kxg.at[mine], kxg.at[mine], kxg_ss.at[k], kxg_rs.at[k], peer) for _, peer, k in plane])
     done(live)
     for p in range(NZL):
         r = (p // 2) * 8
         c = (p % 2) * 128
-        y_send[0, r : r + 8, c : c + 128] = zg[p].astype(BF16)
-    yg[y] = y_send[0]
-    live = go([
-        copy(y_send.at[0], yg.at[y], yg_ss.at[k], yg_rs.at[k], at(x, p, z, core)) for p, k in y_peers
-    ])
-    done(live)
-    live = go([
-        copy(yg, xg.at[x], xg_ss.at[k], xg_rs.at[k], at(p, y, z, core)) for p, k in x_peers
-    ])
-    xg[x] = yg[...]
-    done(live)
-    live = go([copy(xg, cg, cg_ss, cg_rs, other)])
+        out[r : r + 8, c : c + 128] = zg[p].astype(BF16)
+    live = go([copy(out, xg.at[mine], xg_ss.at[k], xg_rs.at[k], peer) for _, peer, k in plane])
+    relay = go([copy(out, cg.at[mine], cg_ss.at[0], cg_rs.at[0], other)])
+    xg[mine] = out[...]
     done(klive)
-    for q in range(NX):
-        for p in range(NY):
-            r = (p // 2) * 8
-            c = (p % 2) * 128
-            ko_ref[q, r : r + 8, c : c + 128] = kxg[q, p]
-    rows = yg.shape[1]
-    for q in range(NX):
-        for p in range(NY):
-            lo = (q * NY + p) * rows
-            wo_ref[pl.ds(pl.multiple_of(core * half + lo, rows), rows)] = xg[q, p].astype(F32)
-    done(live)
-    for q in range(NX):
-        for p in range(NY):
-            lo = (q * NY + p) * rows
-            wo_ref[pl.ds(pl.multiple_of((1 - core) * half + lo, rows), rows)] = cg[q, p].astype(F32)
+    for d in range(n):
+        r, c = (d // 2) % 2 * 8, d % 2 * 128
+        ko_ref[d // 4, r : r + 8, c : c + 128] = kxg[d]
+    for got, (d, k) in zip(live, senders):
+        got.wait_recv()
+        relay += go([copy(xg.at[d], cg.at[d], cg_ss.at[k], cg_rs.at[k], other)])
+    for got in live:
+        got.wait_send()
+    for d in range(n):
+        wo_ref[pl.ds(pl.multiple_of(core * half + d * rows, rows), rows)] = xg[d].astype(F32)
+    done(relay)
+    for d in range(n):
+        wo_ref[pl.ds(pl.multiple_of((1 - core) * half + d * rows, rows), rows)] = cg[d].astype(F32)
 
 
 def reduce_params(wgrad, kgrad):
@@ -162,7 +134,9 @@
     taps = kgrad.shape[1]
     rows = layers * depth
     k_pad = jnp.pad(kgrad, ((0, 0), (0, 16 - taps), (0, 0)))
-    rx, ry = rows // (NC * NX), rows // (NC * NX * NY)
+    n = NX * NY
+    block = (n, rows // (NC * n), channels)
+    tiles = (n, 8, 128)
     V = pltpu.VMEM
     D = pltpu.SemaphoreType.DMA
     w, k = pl.pallas_call(
@@ -174,18 +148,12 @@
         in_specs=[pl.BlockSpec(memory_space=V)] * 2,
         out_specs=(pl.BlockSpec(memory_space=V),) * 2,
         scratch_shapes=[
-            V((NC, rows // NC, channels), BF16), V((rows // NC, channels), BF16),
-            V((NX, rx, channels), BF16), V((NX, rx, channels), BF16),
-            V((NY, ry, channels), BF16), V((NY, ry, channels), BF16),
-            V((NZL, 2, 8, 128), F32), V((NZ, 2, 8, 128), F32),
-            V((NZL, 8, 128), F32), V((NY, ry, channels), BF16),
-            V((NX, NY, ry, channels), BF16), V((NX, NY, ry, channels), BF16),
-            V(k_pad.shape, F32), V(k_pad.shape, F32), V(k_pad.shape, F32),
-            V((NY, 8, 128), F32), V((NY, 8, 128), F32), V((NY, 8, 128), F32),
-            V((NX, NY, 8, 128), F32),
-            D, D, D((NX,)), D((NX,)), D((NY,)), D((NY,)), D((NZ,)), D((NZ,)), D((NZL,)), D((NZL,)),
-            D, D, D((NX,)), D((NX,)), D((NY,)), D((NY,)), D((NY,)), D((NY,)), D((NX,)), D((NX,)),
-            D((NY,)), D((NY,)), D((NX,)), D((NX,)), D, D,
+            V((NC,) + block, BF16), V(block, BF16), V(block, BF16), V(block, BF16),
+            V((NZL, 2, 8, 128), F32), V((NZ, 2, 8, 128), F32), V((NZL, 8, 128), F32),
+            V(block[1:], BF16), V(block, BF16), V(block, BF16),
+            V(k_pad.shape, F32), V(tiles, F32), V(tiles, F32), V(tiles, F32),
+            D((n,)), D((n,)), D((n,)), D((n,)), D((NZ,)), D((NZ,)), D((NZL,)), D((NZL,)),
+            D, D, D((n,)), D((n,)), D((n,)), D((n,)), D((n,)), D((n,)), D((n,)), D((n,)),
         ],
         compiler_params=pltpu.CompilerParams(collective_id=0, has_side_effects=True),
         name="param_sum",
@@ -194,8 +162,8 @@
 
 
 def route_kernel(
-    send_ref, base_ref, seed_ref, wide_ref, seed_out, cells_ref,
-    r1, perm, z_send, r2, tile, strip, seed_strip, h_row, h_col, s_row, s_mid, s_end,
+    obs_ref, to_ref, cell_ref, base_ref, seed_ref, wide_ref, seed_out, cells_ref, place_ref,
+    send_ref, r1, perm, z_send, r2, tile, strip, seed_strip, h_row, h_col, s_row, s_mid, s_end,
     p_ss, p_rs, z_ss, z_rs, h_ss, h_rs, s_ss, s_rs,
 ):
     lon = lax.axis_index("lon")
@@ -229,6 +197,47 @@
     seed = seed_ref[...].astype(F32)
     seed_strip[0] = seed[:, :8].reshape(rows * 8, channels).astype(BF16)
     seed_strip[1] = seed[:, cols - 8 :].reshape(rows * 8, channels).astype(BF16)
+    total = perm.shape[0]
+    items = total // (NX * NY * NZL)
+    i = lax.broadcasted_iota(jnp.int32, (total, 1), 0)
+    pz = i // (items * NX * NY)
+    rest = i - pz * (items * NX * NY)
+    source = (rest % (NX * NY)) * (items * NZL) + (rest // (NX * NY)) * NZL + pz
+    j = lax.broadcasted_iota(jnp.int32, (total, total), 1)
+    perm[...] = jnp.where(j == source, 1.0, 0.0).astype(BF16)
+    count = obs_ref.shape[0]
+    sub = lax.broadcasted_iota(jnp.int32, (count, count), 0)
+    lanes = lax.broadcasted_iota(jnp.int32, (count, count), 1)
+
+    def column(row):
+        return jnp.sum(jnp.where(sub == lanes, row.astype(F32), 0.0), axis=1, keepdims=True)
+
+    def lane_of(width):
+        return lax.broadcasted_iota(jnp.int32, (count, width), 1).astype(F32)
+
+    def picks(index, width):
+        return jnp.where(index == lane_of(width), 1.0, 0.0).astype(BF16)
+
+    group = NX * NY
+    spatial = group * NZL
+    to = column(to_ref[...])
+    cell = column(cell_ref[...])
+    matches = picks(to, spatial)
+    before = jnp.where(sub > lanes, 1.0, 0.0).astype(BF16)
+    ahead = jnp.dot(before, matches, preferred_element_type=F32)
+    position = jnp.sum(ahead * matches.astype(F32), axis=1, keepdims=True)
+    far = jnp.floor(to * (1.0 / group))
+    start = (to - far * group) * (items * NZL) + far
+    cell_rows = jnp.where(position == lane_of(channels), cell + 1.0, 0.0).astype(BF16)
+    place_ref[...] = picks(to * (items - 1) + position, spatial * (items - 1))
+    turn = (((0,), (0,)), ((), ()))
+    packed = lax.dot_general(picks(start + position * NZL, total), obs_ref[...], turn, preferred_element_type=F32)
+    packed = packed + lax.dot_general(
+        picks(start + (items - 1) * NZL, total), cell_rows, turn, preferred_element_type=F32
+    )
+    packed = packed.reshape(group, items * NZL, channels)
+    item = lax.broadcasted_iota(jnp.int32, packed.shape, 1)
+    send_ref[...] = jnp.where(item >= (items - 1) * NZL, packed - 1.0, packed).astype(BF16)
     pl.semaphore_wait(barrier, len(greeted))
 
     def copy(src, dst, ss, rs, peer):
@@ -262,14 +271,6 @@
         ]
     go(seeds)
     r1[mine] = send_ref[mine]
-    total = perm.shape[0]
-    items = total // (NX * NY * NZL)
-    i = lax.broadcasted_iota(jnp.int32, (total, 1), 0)
-    pz = i // (items * NX * NY)
-    rest = i - pz * (items * NX * NY)
-    source = (rest % (NX * NY)) * (items * NZL) + (rest // (NX * NY)) * NZL + pz
-    j = lax.broadcasted_iota(jnp.int32, (total, total), 1)
-    perm[...] = jnp.where(j == source, 1.0, 0.0).astype(BF16)
     done(live)
     flat = r1[...].astype(F32).reshape(total, channels).astype(BF16)
     z_send[...] = (
@@ -278,8 +279,6 @@
     live = go([copy(z_send.at[p], r2.at[zl], z_ss.at[k], z_rs.at[k], peer) for p, peer, k in along])
     r2[zl] = z_send[zl]
     done(live)
-    group = NX * NY
-    spatial = group * NZL
     n_cells = rows * cols
     cells = r2[:, (items - 1) * group : items * group].reshape(spatial, channels)
     cells_ref[...] = cells
@@ -291,7 +290,6 @@
     for p in range(items - 1):
         hot = jnp.where(cells[:, p : p + 1] == lane, 1.0, 0.0).astype(BF16)
         vals = r2[:, p * group : (p + 1) * group].reshape(spatial, channels)
-        turn = (((0,), (0,)), ((), ()))
         summed = summed + lax.dot_general(hot, vals, turn, preferred_element_type=F32)
         counts = counts + lax.dot_general(hot, ones, turn, preferred_element_type=F32)
     base = base_ref[...].astype(F32).reshape(n_cells, channels)
@@ -338,10 +336,11 @@
         put(wide_ref, 2 * rows + r, left[2][c : c + 8], h_row[1, r], right[2][c : c + 8], has_south)
 
 
-def route(send, base, seed, edge):
+def route(values, to, cell, base, seed, edge, cap):
     rows, cols, channels = base.shape
     spatial = NX * NY * NZL
-    items = send.shape[1] // NZL
+    items = cap + 1
+    send_shape = (NX * NY, items * NZL, channels)
     V = pltpu.VMEM
     D = pltpu.SemaphoreType.DMA
     return pl.pallas_call(
@@ -350,11 +349,12 @@
             jax.ShapeDtypeStruct((3 * rows, cols + 16, channels), BF16),
             jax.ShapeDtypeStruct((2 * edge + rows, cols + 16, channels), BF16),
             jax.ShapeDtypeStruct((spatial, channels), BF16),
+            jax.ShapeDtypeStruct((values.shape[0], spatial * cap), BF16),
         ),
-        in_specs=[pl.BlockSpec(memory_space=V)] * 3,
-        out_specs=(pl.BlockSpec(memory_space=V),) * 3,
+        in_specs=[pl.BlockSpec(memory_space=V)] * 5,
+        out_specs=(pl.BlockSpec(memory_space=V),) * 4,
         scratch_shapes=[
-            V(send.shape, BF16), V((items * spatial, items * spatial), BF16),
+            V(send_shape, BF16), V(send_shape, BF16), V((items * spatial, items * spatial), BF16),
             V((NZL, items * NX * NY, channels), BF16), V((NZL, items * NX * NY, channels), BF16),
             V(base.shape, BF16), V((2, rows * 8, channels), BF16), V((2, rows * 8, channels), BF16),
             V((2, rows, cols, channels), BF16), V((2, 3, rows * 8, channels), BF16),
@@ -364,7 +364,7 @@
         ],
         compiler_params=pltpu.CompilerParams(collective_id=1, has_side_effects=True),
         name="route",
-    )(send, base, seed)
+    )(values, to, cell, base, seed)
 
 
 def depthwise(padded, kernel_rows, offset, sign):
@@ -405,28 +405,9 @@
         row = row + lax.axis_index("lat") * lat_rows - radius
         return jnp.where((row >= 0) & (row < n_lat * lat_rows), v, jnp.zeros((), v.dtype))
 
-    target = obs_tile[0, :, 0]
-    matches = (target[:, None] == jnp.arange(spatial, dtype=jnp.int32)[None, :]).astype(BF16)
-    order = jnp.arange(obs_count, dtype=jnp.int32)
-    before = (order[:, None] > order[None, :]).astype(BF16)
-    ahead = jnp.dot(before, matches, preferred_element_type=F32)
-    position = jnp.sum(ahead * matches.astype(F32), axis=1).astype(jnp.int32)
-    slot_of = target * cap + position
-    place = (slot_of[:, None] == jnp.arange(spatial * cap, dtype=jnp.int32)[None, :]).astype(BF16)
-    send_values = lax.dot_general(
-        place, obs_values[0], (((0,), (0,)), ((), ())), preferred_element_type=F32
-    ).astype(BF16)
-    lane = jnp.arange(channels, dtype=jnp.int32)[None, :]
-    cell_rows = jnp.where(position[:, None] == lane, obs_cell[0][:, None] + 1, 0).astype(BF16)
-    send_cells = (
-        lax.dot_general(matches, cell_rows, (((0,), (0,)), ((), ())), preferred_element_type=F32) - 1.0
-    ).astype(BF16)
-    packed = jnp.concatenate(
-        [send_values.reshape(spatial, cap, channels), send_cells.reshape(spatial, 1, channels)], axis=1
-    )
-    send = packed.reshape(NZL, NX * NY, cap + 1, channels).transpose(1, 2, 0, 3)
-    send = send.reshape(NX * NY, (cap + 1) * NZL, channels)
-    hidden, seed_wide, cell_out = route(send, backdrop[0], seed_grad[0], n_layers)
+    hidden, seed_wide, cell_out, place = route(
+        obs_values[0], obs_tile.reshape(1, obs_count), obs_cell, backdrop[0], seed_grad[0], n_layers, cap
+    )
     seed_wide = seed_wide[:, 8 - n_layers : 8 + lon_cols + n_layers]
     recv_cells = cell_out[:, :cap].astype(jnp.int32).reshape(spatial * cap)
     onehot_mask = recv_cells[None, :] == jnp.arange(n_cells, dtype=jnp.int32)[:, None]

time: 150 us -> 141 us (0.940)
  Pallas kernels: 103 us -> 98.9 us
  other arithmetic: 15 us -> 12.3 us
  matrix products: 13.9 us -> 11.5 us
    pallas_call x1, Pallas kernels: 56.7 us -> 52.3 us  [reduce_params(): pl.pallas_call(reduce_kernel, out_shape=(jax.ShapeDtypeStruct((rows, chan...]
    dot_general x3 -> x0, matrix products: 2.34 us -> none  [the longest x1 0.98 us: on_device(): ahead = jnp.dot(before, matches, preferred_element_type=F32)]
    unnamed x40 -> x36, local copies, waits for them, and re-layouts: 4.71 us -> 4.94 us
  transfers between devices with their start and end apart: 1 -> 1, of which waited for: 0 -> 0; matrix products, arithmetic and copies ran while one was open for 9% -> 10% of each run, Pallas kernels for 38% -> 37%
where the time goes in v3:
time: 141 us; the launch traced here: 140 us
  Pallas kernels  98.9 us (70%)
  other arithmetic  12.3 us (9%)
  matrix products  11.5 us (8%)
  starting transfers between devices  8.79 us (6%)
  local copies, waits for them, and re-layouts  7.83 us (6%)
    pallas_call x1, Pallas kernels, reduce_params(): pl.pallas_call(reduce_kernel, out_shape=(jax.ShapeDtypeStruct((rows, chan...  52.3 us
    pallas_call x1, Pallas kernels, route(): pl.pallas_call(route_kernel, out_shape=(jax.ShapeDtypeStruct((3 * rows, c...  46.6 us
    all_to_all x1, starting transfers between devices, on_device(): lax.all_to_all(slot_grad.reshape(spatial, 1, cap, channels), ('lon', 'lat...  8.79 us
    dot_general x4, matrix products, on_device(): lax.dot_general(acts[l], crop(grad_bf, radius).reshape(n_cells, channels)...  6.09 us
    unnamed x36, local copies, waits for them, and re-layouts  4.94 us
    convert_element_type x4, other arithmetic, on_device(): act = jax.nn.silu(pre).astype(BF16)  4.08 us
  transfers between devices with their start and end apart: 1, of which 0 were waited for; matrix products, arithmetic and copies ran while one was open for 10% of the time, Pallas kernels for 37%

profile of v3, /device:TPU:1, one launch (start us, length us, event | category | flops | bytes accessed | tf_op | source)
XLA Modules:
  0.0 140.3 jit_solution(17467806303449575445)
XLA Ops:
  0.6 0.9 fusion.109
  1.5 0.9 fusion.108
  2.5 46.6 %route.1 = (bf16[24,48,256]{2,1,0:T(8,128)(2,1)}, bf16[16,48,256]{2,1,0:T(8,128)(2,1)}, bf16[128,256]{1,0:T(8,128)(2,1)}, bf16[256,512]{1,0:T(8,128)(2,1)}) custom-call(bf16[256,256]{1,0:T(8,128)(2,1)} %bitcast.142, s32[1,256]{1,0:T(1,128)} %bitcast.258, s32[1,256]{1,0:T(1,128)} %cell_ref.1, bf16[8,32,256]{2,1,0:T(8,128)(2,1)} %bitcast.143, ...), custom_call_target="tpu_custom_call" | custom-call | tf_op jit(solution)/shard_map/route/pallas_call | solution.py:346
  49.2 1.9 %convert_multiply_fusion.40 = (f32[16,40,256]{2,1,0:T(8,128)S(1)}, bf16[16,40,256]{2,1,0:T(8,128)(2,1)}) fusion(bf16[16,48,256]{2,1,0:T(8,128)(2,1)} %get-tuple-element.11), kind=kLoop, calls=%fused_computation.90 | loop fusion | flops 491520 | bytes 1310720 | tf_op jit(solution)/shard_map/mul | solution.py:435
  51.1 0.1 reshape.244
  51.2 0.1 convert_reduce_fusion
  51.3 1.1 multiply_convert_fusion
  52.4 0.3 fusion.3
  52.8 0.4 copy-done.3
  53.2 1.0 multiply_convert_fusion.1
  54.2 0.3 fusion.4
  54.5 0.4 copy-done.4
  55.0 0.9 multiply_convert_fusion.2
  55.9 0.3 fusion.6
  56.2 1.5 %add_divide_fusion = (f32[16,40,256]{2,1,0:T(8,128)}, f32[16,40,256]{2,1,0:T(8,128)S(1)}) fusion(bf16[18,42,256]{2,1,0:T(8,128)(2,1)S(1)} %fusion.6, f32[256]{0:T(256)S(1)} %bitcast.188, f32[256]{0:T(256)S(1)} %bitcast.186, f32[256]{0:T(256)S(1)} %bitcast.192, f32[256]{0:T(256)S(1)} %bitcast.194, f32[256]{0:T(256)S(1)} %bitcast.196, f32[256]{0:T(256)S(1)} %bitcast.198, ...), kind=kLoop, calls=%fused_computation.91 | loop fusion | flops 4751360 | bytes 4269056 | tf_op jit(solution)/shard_map/jit(silu)/div | solution.py:422
  57.6 0.4 fusion.9
  58.1 0.4 copy-done.1
  58.5 0.6 fusion.104
  59.0 0.4 fusion.11
  59.4 0.3 copy-done.6
  59.8 0.5 fusion.103
  60.3 0.3 fusion.12
  60.6 0.3 copy-done.11
  60.9 0.4 fusion.102
  61.4 0.3 fusion.13
  61.7 0.4 copy-done.13
  62.0 0.2 fusion.73
  62.3 0.1 fusion.75
  62.4 0.3 convolution_convert_fusion
  62.8 0.8 reshape.242
  63.5 8.8 %all-to-all-start = ((bf16[128,1,4,256]{3,2,1,0:T(4,128)(2,1)}), bf16[128,1,4,256]{3,2,1,0:T(4,128)(2,1)S(1)}, u32[]{:S(2)}, u32[]{:S(2)}) async-start(bf16[128,1,4,256]{3,2,1,0:T(4,128)(2,1)} %bitcast.141), calls=%async_computation | async-start | bytes 524288 | tf_op jit(solution)/shard_map/all_to_all | solution.py:469
  72.4 2.0 %convolution_bitcast_fusion.1 = f32[1,256,256]{2,1,0:T(8,128)} fusion(bf16[14,38,256]{2,1,0:T(8,128)(2,1)} %copy-done.6, bf16[18,42,256]{2,1,0:T(8,128)(2,1)} %copy-done.5), kind=kOutput, calls=%fused_computation.24 | convolution fusion | flops 33554432 | bytes 524288 | tf_op jit(solution)/shard_map/dot_general | solution.py:441
  74.3 1.8 %convolution_bitcast_fusion.2 = f32[1,256,256]{2,1,0:T(8,128)} fusion(bf16[12,36,256]{2,1,0:T(8,128)(2,1)S(1)} %copy-done.12, bf16[20,44,256]{2,1,0:T(8,128)(2,1)} %copy-done.4), kind=kOutput, calls=%fused_computation.25 | convolution fusion | flops 33554432 | bytes 524288 | tf_op jit(solution)/shard_map/dot_general | solution.py:441
  76.2 0.3 fusion.58
  76.5 0.3 fusion.49
  76.8 0.3 fusion.40
  77.1 0.3 fusion.67
  77.5 0.6 select_maximum_fusion.k_ref
  78.2 1.1 convolution_bitcast_fusion.3
  79.3 1.2 fusion.74
  80.5 1.1 convolution_bitcast_fusion
  81.7 1.0 pad_maximum_fusion
  82.7 52.3 %param_sum.1 = (f32[1024,256]{1,0:T(8,128)}, f32[4,16,256]{2,1,0:T(8,128)}) custom-call(f32[1024,256]{1,0:T(8,128)} %bitcast.139, f32[4,16,256]{2,1,0:T(8,128)} %select_maximum_fusion.k_ref), custom_call_target="tpu_custom_call" | custom-call | tf_op jit(solution)/shard_map/param_sum/pallas_call | solution.py:142
  135.0 1.6 %copy.16 = f32[4,9,256]{2,0,1:T(4,128)} copy(f32[4,9,256]{2,1,0:T(8,128)} %bitcast.145) | data formatting | bytes 73728
  136.6 1.8 %fusion.16 = bf16[1,8,32,256]{3,2,1,0:T(8,128)(2,1)} fusion(bf16[8,32,256]{2,1,0:T(8,128)(2,1)S(1)} %fusion.74, bf16[18,42,256]{2,1,0:T(8,128)(2,1)S(1)} %fusion.6, bf16[4,256,256]{2,1,0:T(8,128)(2,1)} %param.13), kind=kOutput, calls=%fused_computation.32 | convolution fusion | flops 33751040 | bytes 524288 | tf_op jit(solution)/shard_map/dot_general | solution.py:429
  138.3 0.1 reshape.243
  138.4 0.9 fusion.15
  139.3 1.0 copy.18
  (42 shorter events, 0.3 us)
Async XLA Ops:
  49.1 1.9 %copy-start.15 = (bf16[128,256]{1,0:T(8,128)(2,1)S(1)}, bf16[128,256]{1,0:T(8,128)(2,1)}, u32[]{:S(2)}) copy-start(bf16[128,256]{1,0:T(8,128)(2,1)} %get-tuple-element.15) | copy-start | bytes 196612
  49.2 2.2 %copy-start = (bf16[24,48,256]{2,1,0:T(8,128)(2,1)S(1)}, bf16[24,48,256]{2,1,0:T(8,128)(2,1)}, u32[]{:S(2)}) copy-start(bf16[24,48,256]{2,1,0:T(8,128)(2,1)} %get-tuple-element.10) | copy-start | bytes 1769476
  51.3 1.1 copy-start.16
  52.4 0.8 copy-start.3
  54.2 0.8 copy-start.4
  55.8 1.8 %copy-start.5 = (bf16[18,42,256]{2,1,0:T(8,128)(2,1)}, bf16[18,42,256]{2,1,0:T(8,128)(2,1)S(1)}, u32[]{:S(2)}) copy-start(bf16[18,42,256]{2,1,0:T(8,128)(2,1)S(1)} %get-tuple-element.76) | copy-start | bytes 1161220
  56.2 1.5 %copy-start.7 = (bf16[16,48,256]{2,1,0:T(8,128)(2,1)S(1)}, bf16[16,48,256]{2,1,0:T(8,128)(2,1)}, u32[]{:S(2)}) copy-start(bf16[16,48,256]{2,1,0:T(8,128)(2,1)} %get-tuple-element.11) | copy-start | bytes 1179652
  57.6 0.8 copy-start.1
  59.0 0.7 copy-start.6
  60.2 0.7 copy-start.11
  61.4 0.7 copy-start.13
  63.5 74.8 %all-to-all-start = ((bf16[128,1,4,256]{3,2,1,0:T(4,128)(2,1)}), bf16[128,1,4,256]{3,2,1,0:T(4,128)(2,1)S(1)}, u32[]{:S(2)}, u32[]{:S(2)}) async-start(bf16[128,1,4,256]{3,2,1,0:T(4,128)(2,1)} %bitcast.141), calls=%async_computation | async-start | bytes 524288 | tf_op jit(solution)/shard_map/all_to_all | solution.py:469
  72.3 2.0 %copy-start.12 = (bf16[12,36,256]{2,1,0:T(8,128)(2,1)S(1)}, bf16[12,36,256]{2,1,0:T(8,128)(2,1)}, u32[]{:S(2)}) copy-start(bf16[12,36,256]{2,1,0:T(8,128)(2,1)} %copy-done.11) | copy-start | bytes 663556
  77.1 1.1 copy-start.14
  79.3 2.4 %copy-start.9 = (f32[1,256,256]{2,1,0:T(8,128)S(1)}, f32[1,256,256]{2,1,0:T(8,128)}, u32[]{:S(2)}) copy-start(f32[1,256,256]{2,1,0:T(8,128)} %convolution_bitcast_fusion.1) | copy-start | bytes 786436
  79.3 2.4 %copy-start.10 = (f32[1,256,256]{2,1,0:T(8,128)S(1)}, f32[1,256,256]{2,1,0:T(8,128)}, u32[]{:S(2)}) copy-start(f32[1,256,256]{2,1,0:T(8,128)} %convolution_bitcast_fusion.2) | copy-start | bytes 786436
  82.7 55.7 %copy-start.8 = (bf16[256,512]{1,0:T(8,128)(2,1)S(1)}, bf16[256,512]{1,0:T(8,128)(2,1)}, u32[]{:S(2)}) copy-start(bf16[256,512]{1,0:T(8,128)(2,1)} %get-tuple-element.14) | copy-start | bytes 786436
  135.0 4.3 %copy-start.2 = (f32[1024,256]{1,0:T(8,128)S(1)}, f32[1024,256]{1,0:T(8,128)}, u32[]{:S(2)}) copy-start(f32[1024,256]{1,0:T(8,128)} %get-tuple-element.12) | copy-start | bytes 3145732

commit v4 on v3

v4 whole, which is shorter than its diff:
```python
import functools

import jax
import jax.numpy as jnp
from jax import lax
from jax.experimental import pallas as pl
from jax.experimental.pallas import tpu as pltpu
from jax.sharding import PartitionSpec as P

F32 = jnp.float32
BF16 = jnp.bfloat16
MESH = pl.DeviceIdType.MESH
NX, NY, NZL, NZH, NC = 4, 4, 8, 2, 2
NZ = NZL * NZH


def whole_kernel(
    scale, obs_ref, to_ref, cell_ref, base_ref, seed_ref, k_ref, w_ref,
    state_ref, wo_ref, ko_ref, grad_ref,
    send_ref, r1, perm, z_send, r2, tile, strip, seed_strip, h_row, h_col, s_row, s_mid, s_end,
    place, back, hots, count_ref, hs, ds, ub, own, gs, es, wg, kg, rz_send, rz_recv, rp_send, rp_recv,
    c_send, c_recv, x_send, x_recv, q_send, q_recv, zg, out, xg, cg, kc_recv, kx_send, kx_recv, kxg,
    p_ss, p_rs, z_ss, z_rs, h_ss, h_rs, s_ss, s_rs, b_ss, b_rs, o_ss, o_rs,
    c_ss, c_rs, x_ss, x_rs, q_ss, q_rs, g_ss, g_rs,
    kc_ss, kc_rs, kx_ss, kx_rs, kxg_ss, kxg_rs, xg_ss, xg_rs, cg_ss, cg_rs,
):
    lon = lax.axis_index("lon")
    x = lax.axis_index("lat")
    ens = lax.axis_index("ens")
    n_lon = lax.axis_size("lon")
    zl, y = lon // NY, lon % NY
    mine = y * NX + x

    def at(plon, px):
        return {"lon": plon, "lat": px, "ens": ens}

    plane = []
    for k in range(1, NX * NY):
        px, py = (x + k % NX) % NX, (y + k // NX) % NY
        plane.append((py * NX + px, at(zl * NY + py, px), k))
    along = []
    for k in range(1, NZL):
        pz = (zl + k) % NZL
        along.append((pz, at(pz * NY + y, x), k))
    west, east = (lon + n_lon - 1) % n_lon, (lon + 1) % n_lon
    north, south = (x + NX - 1) % NX, (x + 1) % NX
    lats = (south, x, north)

    barrier = pltpu.get_barrier_semaphore()
    zh, core = ens // NC, ens % NC
    z = zh * NZL + zl

    def dev(pz, pc):
        return {"lon": (pz % NZL) * NY + y, "lat": x, "ens": (pz // NZL) * NC + pc}

    partner = dev(z, 1 - core)
    z_peers = [((z + k) % NZ, k) for k in range(1, NZ)]
    greeted = [partner] + [p for _, p, _ in plane] + [dev(p, core) for p, _ in z_peers]
    greeted += [at(lon, north), at(lon, south)] + [at(w, q) for w in (west, east) for q in lats]
    for peer in greeted:
        pl.semaphore_signal(barrier, inc=1, device_id=peer, device_id_type=MESH)
    rows, cols, channels = base_ref.shape
    seed = seed_ref[...].astype(F32)
    seed_strip[0] = seed[:, :8].reshape(rows * 8, channels).astype(BF16)
    seed_strip[1] = seed[:, cols - 8 :].reshape(rows * 8, channels).astype(BF16)
    total = perm.shape[0]
    items = total // (NX * NY * NZL)
    i = lax.broadcasted_iota(jnp.int32, (total, 1), 0)
    pz = i // (items * NX * NY)
    rest = i - pz * (items * NX * NY)
    source = (rest % (NX * NY)) * (items * NZL) + (rest // (NX * NY)) * NZL + pz
    j = lax.broadcasted_iota(jnp.int32, (total, total), 1)
    perm[...] = jnp.where(j == source, 1.0, 0.0).astype(BF16)
    count = obs_ref.shape[0]
    sub = lax.broadcasted_iota(jnp.int32, (count, count), 0)
    lanes = lax.broadcasted_iota(jnp.int32, (count, count), 1)

    def column(row):
        return jnp.sum(jnp.where(sub == lanes, row.astype(F32), 0.0), axis=1, keepdims=True)

    def lane_of(width):
        return lax.broadcasted_iota(jnp.int32, (count, width), 1).astype(F32)

    def picks(index, width):
        return jnp.where(index == lane_of(width), 1.0, 0.0).astype(BF16)

    group = NX * NY
    spatial = group * NZL
    to = column(to_ref[...])
    cell = column(cell_ref[...])
    matches = picks(to, spatial)
    before = jnp.where(sub > lanes, 1.0, 0.0).astype(BF16)
    ahead = jnp.dot(before, matches, preferred_element_type=F32)
    position = jnp.sum(ahead * matches.astype(F32), axis=1, keepdims=True)
    far = jnp.floor(to * (1.0 / group))
    start = (to - far * group) * (items * NZL) + far
    cell_rows = jnp.where(position == lane_of(channels), cell + 1.0, 0.0).astype(BF16)
    place[...] = picks(
        (to - far * group) * ((items - 1) * NZL) + position * NZL + far, spatial * (items - 1)
    )
    slots = back.shape[0]
    i = lax.broadcasted_iota(jnp.int32, (slots, 1), 0)
    each = (items - 1) * NZL
    source = (i % NZL) * (slots // NZL) + (i % each) // NZL * group + i // each
    j = lax.broadcasted_iota(jnp.int32, (slots, slots), 1)
    back[...] = jnp.where(j == source, 1.0, 0.0).astype(BF16)
    turn = (((0,), (0,)), ((), ()))
    packed = lax.dot_general(picks(start + position * NZL, total), obs_ref[...], turn, preferred_element_type=F32)
    packed = packed + lax.dot_general(
        picks(start + (items - 1) * NZL, total), cell_rows, turn, preferred_element_type=F32
    )
    packed = packed.reshape(group, items * NZL, channels)
    item = lax.broadcasted_iota(jnp.int32, packed.shape, 1)
    send_ref[...] = jnp.where(item >= (items - 1) * NZL, packed - 1.0, packed).astype(BF16)
    pl.semaphore_wait(barrier, len(greeted))

    def copy(src, dst, ss, rs, peer):
        return pltpu.make_async_remote_copy(
            src_ref=src, dst_ref=dst, send_sem=ss, recv_sem=rs, device_id=peer, device_id_type=MESH
        )

    def go(copies):
        for c in copies:
            c.start()
        return copies

    def done(copies):
        for c in copies:
            c.wait()

    live = go([copy(send_ref.at[d], r1.at[mine], p_ss.at[k], p_rs.at[k], peer) for d, peer, k in plane])
    edge = s_row.shape[1]
    cut = edge * 8
    seeds = [
        copy(seed_ref.at[rows - edge : rows], s_row.at[0], s_ss.at[0], s_rs.at[0], at(lon, south)),
        copy(seed_ref.at[0:edge], s_row.at[1], s_ss.at[1], s_rs.at[1], at(lon, north)),
    ]
    for side, other in ((0, east), (1, west)):
        src = seed_strip.at[1 - side]
        n = 2 + 3 * side
        seeds += [
            copy(src.at[rows * 8 - cut : rows * 8], s_end.at[side, 0], s_ss.at[n], s_rs.at[n], at(other, south)),
            copy(src, s_mid.at[side], s_ss.at[n + 1], s_rs.at[n + 1], at(other, x)),
            copy(src.at[0:cut], s_end.at[side, 1], s_ss.at[n + 2], s_rs.at[n + 2], at(other, north)),
        ]
    go(seeds)
    r1[mine] = send_ref[mine]
    done(live)
    flat = r1[...].astype(F32).reshape(total, channels).astype(BF16)
    z_send[...] = (
        jnp.dot(perm[...], flat, preferred_element_type=F32).astype(BF16).reshape(z_send.shape)
    )
    live = go([copy(z_send.at[p], r2.at[zl], z_ss.at[k], z_rs.at[k], peer) for p, peer, k in along])
    r2[zl] = z_send[zl]
    done(live)
    n_cells = rows * cols
    cells = r2[:, (items - 1) * group : items * group].reshape(spatial, channels)
    cells = cells.astype(F32)
    lane = lax.broadcasted_iota(jnp.int32, (spatial, n_cells), 1).astype(F32)
    ones = jnp.ones((spatial, channels), BF16)
    summed = jnp.zeros((n_cells, channels), F32)
    counts = jnp.zeros((n_cells, channels), F32)
    for p in range(items - 1):
        hot = jnp.where(cells[:, p : p + 1] == lane, 1.0, 0.0).astype(BF16)
        hots[p] = hot
        vals = r2[:, p * group : (p + 1) * group].reshape(spatial, channels)
        summed = summed + lax.dot_general(hot, vals, turn, preferred_element_type=F32)
        counts = counts + lax.dot_general(hot, ones, turn, preferred_element_type=F32)
    count_ref[...] = counts
    base = base_ref[...].astype(F32).reshape(n_cells, channels)
    h0 = (base + summed / jnp.maximum(counts, 1.0)).reshape(rows, cols, channels)
    tile[...] = h0.astype(BF16)
    strip[0] = h0[:, :8].reshape(rows * 8, channels).astype(BF16)
    strip[1] = h0[:, cols - 8 :].reshape(rows * 8, channels).astype(BF16)
    halos = []
    for side, other in ((0, east), (1, west)):
        for t, q in enumerate(lats):
            n = 2 + 3 * side + t
            halos.append(copy(strip.at[1 - side], h_col.at[side, t], h_ss.at[n], h_rs.at[n], at(other, q)))
    halos += [
        copy(tile, h_row.at[0], h_ss.at[0], h_rs.at[0], at(lon, south)),
        copy(tile, h_row.at[1], h_ss.at[1], h_rs.at[1], at(lon, north)),
    ]
    go(halos)
    done(seeds)

    def put(dst, row, left, mid, right, keep):
        line = jnp.concatenate([left.astype(F32), mid.astype(F32), right.astype(F32)], axis=0)
        if keep is not None:
            line = jnp.where(keep, line, 0.0)
        dst[row] = line if dst is not gs else line * scale

    has_north, has_south = x > 0, x < NX - 1
    for r in range(edge):
        c = r * 8
        put(gs, r, s_end[0, 0].astype(F32)[c : c + 8], s_row[0, r], s_end[1, 0].astype(F32)[c : c + 8], has_north)
        put(
            gs, edge + rows + r,
            s_end[0, 1].astype(F32)[c : c + 8], s_row[1, r], s_end[1, 1].astype(F32)[c : c + 8], has_south,
        )
    for r in range(rows):
        c = r * 8
        put(gs, edge + r, s_mid[0].astype(F32)[c : c + 8], seed[r], s_mid[1].astype(F32)[c : c + 8], None)
    done(halos)
    first_h = hs.at[0]
    left = [h_col[0, t].astype(F32) for t in range(3)]
    right = [h_col[1, t].astype(F32) for t in range(3)]
    for r in range(rows):
        c = r * 8
        put(first_h, r, left[0][c : c + 8], h_row[0, r], right[0][c : c + 8], has_north)
        put(first_h, rows + r, left[1][c : c + 8], tile[r], right[1][c : c + 8], None)
        put(first_h, 2 * rows + r, left[2][c : c + 8], h_row[1, r], right[2][c : c + 8], has_south)

    layers = w_ref.shape[0]
    width = hs.shape[2]
    tall = hs.shape[1]

    def turned(v, by):
        return pltpu.roll(v, by % width, 0)

    def inside(i, v):
        row = x * rows + i
        return jnp.where((row >= 0) & (row < NX * rows), v, 0.0)

    for l in range(layers):
        lo, hi = l + 1, tall - 1 - l
        taps = [k_ref[l, t : t + 1] for t in range(9)]

        def forward(p, _, l=l, taps=taps):
            lines = [hs[l, p + a - 1] for a in range(3)]
            sums = [taps[b] * lines[0] + taps[3 + b] * lines[1] + taps[6 + b] * lines[2] for b in range(3)]
            d = turned(sums[0], 1) + sums[1] + turned(sums[2], -1)
            ds[l, p] = d
            ub[p] = (d / (1.0 + jnp.exp(-d))).astype(BF16)
            return 0

        lax.fori_loop(lo, hi, forward, 0)
        own[l] = ub[rows : 2 * rows].astype(F32)[:, 8 : 8 + cols].reshape(n_cells, channels).astype(BF16)
        if l == layers - 1:
            mixed = jnp.dot(own[l], w_ref[l], preferred_element_type=F32)
            kept = hs[l, rows : 2 * rows][:, 8 : 8 + cols]
            state_ref[...] = (kept + mixed.reshape(rows, cols, channels)).astype(BF16)
        else:
            step = (hi - lo) // 2

            def mix(t, _, l=l, lo=lo, step=step):
                at_row = lo + t * step
                u = ub[pl.ds(at_row, step)].reshape(step * width, channels)
                mixed = jnp.dot(u, w_ref[l], preferred_element_type=F32).reshape(step, width, channels)
                for q in range(step):
                    new = (hs[l, at_row + q] + mixed[q]).astype(BF16).astype(F32)
                    hs[l + 1, at_row + q] = inside(at_row + q - rows, new)
                return 0

            lax.fori_loop(0, 2, mix, 0)
    shift = rows - edge
    for l in reversed(range(layers)):
        radius = l + 1
        lo, hi = edge - radius, edge + rows + radius
        step = (hi - lo) // 2

        def pull(t, _, l=l, lo=lo, step=step):
            at_row = lo + t * step
            b = gs[pl.ds(at_row, step)].reshape(step * width, channels).astype(BF16)
            ga = lax.dot_general(b, w_ref[l], (((1,), (1,)), ((), ())), preferred_element_type=F32)
            ga = ga.reshape(step, width, channels)
            for q in range(step):
                d = ds[l, at_row + q + shift]
                sig = 1.0 / (1.0 + jnp.exp(-d))
                e = (ga[q] * (sig * (1.0 + d * (1.0 - sig)))).astype(BF16).astype(F32)
                es[at_row + q] = inside(at_row + q - edge, e)
            return 0

        lax.fori_loop(0, 2, pull, 0)
        g_own = gs[edge : edge + rows][:, 8 : 8 + cols].reshape(n_cells, channels).astype(BF16)
        wg[l * channels : (l + 1) * channels] = lax.dot_general(
            own[l], g_own, (((0,), (0,)), ((), ())), preferred_element_type=F32
        )
        col = lax.broadcasted_iota(jnp.int32, (width, channels), 0)
        mid = (col >= 8) & (col < 8 + cols)

        def tap_sums(r, acc, l=l):
            e = jnp.where(mid, es[edge + r], 0.0)
            moved = [turned(e, -1), e, turned(e, 1)]
            new = []
            for t in range(9):
                prod = moved[t % 3] * hs[l, rows + r + t // 3 - 1]
                new.append(acc[t] + jnp.sum(prod.reshape(width // 8, 8, channels), axis=0))
            return tuple(new)

        acc = lax.fori_loop(0, rows, tap_sums, tuple(jnp.zeros((8, channels), F32) for _ in range(9)))
        lines = [jnp.sum(v, axis=0, keepdims=True) for v in acc]
        kg[l] = jnp.concatenate(lines + [jnp.zeros((kg.shape[1] - 9, channels), F32)], axis=0)
        taps = [k_ref[l, t : t + 1] for t in range(9)]

        def spread(q, _, taps=taps):
            lines = [es[q + 1 - a] for a in range(3)]
            sums = [taps[b] * lines[0] + taps[3 + b] * lines[1] + taps[6 + b] * lines[2] for b in range(3)]
            gs[q] = gs[q] + turned(sums[0], -1) + sums[1] + turned(sums[2], 1)
            return 0

        lax.fori_loop(edge - l, edge + rows + l, spread, 0)
    cell_grad = gs[edge : edge + rows][:, 8 : 8 + cols].reshape(n_cells, channels)
    cell_grad = (cell_grad / jnp.maximum(count_ref[...], 1.0)).astype(BF16)
    for p in range(items - 1):
        part = jnp.dot(hots[p], cell_grad, preferred_element_type=F32).astype(BF16)
        rz_send[:, p * group : (p + 1) * group] = part.reshape(NZL, group, channels)
    outward = go([copy(rz_send.at[p], rz_recv.at[zl], b_ss.at[k], b_rs.at[k], peer) for p, peer, k in along])
    rz_recv[zl] = rz_send[zl]
    senders = []
    for k in range(1, NX * NY):
        px, py = (x + NX - k % NX) % NX, (y + NY - k // NX) % NY
        senders.append((py * NX + px, k))
    n, prow = c_send.shape[1], c_send.shape[2]
    half = n * prow
    c_send[...] = wg[...].astype(BF16).reshape(c_send.shape)
    order = [(d, k) for d, _, k in plane] + [(mine, 0)]
    first = go([copy(kg, kc_recv, kc_ss, kc_rs, partner)])
    pieces = go([copy(c_send.at[1 - core, d], c_recv.at[d], c_ss.at[k], c_rs.at[k], partner) for d, k in order])
    done(first)
    ksum = kg[...] + kc_recv[...]
    for d in range(n):
        r, c = (d // 2) % 2 * 8, d % 2 * 128
        kx_send[d] = ksum[d // 4, r : r + 8, c : c + 128]
    live = go([copy(kx_send.at[d], kx_recv.at[mine], kx_ss.at[k], kx_rs.at[k], peer) for d, peer, k in plane])
    kx_recv[mine] = kx_send[mine]
    for (d, k), piece in zip(order, pieces):
        piece.wait_recv()
        own = wg[pl.ds(pl.multiple_of(core * half + d * prow, prow), prow)]
        x_send[d] = (own + c_recv[d].astype(F32)).astype(BF16)
        if k:
            live += go([copy(x_send.at[d], x_recv.at[mine], x_ss.at[k], x_rs.at[k], plane[k - 1][1])])
    x_recv[mine] = x_send[mine]
    for piece in pieces:
        piece.wait_send()
    done(live)
    total = x_recv[0].astype(F32)
    ktile = kx_recv[0]
    for q in range(1, n):
        total = total + x_recv[q].astype(F32)
        ktile = ktile + kx_recv[q]
    for p in range(NZL):
        q_send[p, 0] = total[(p // 2) * 8 : (p // 2) * 8 + 8, (p % 2) * 128 : (p % 2) * 128 + 128]
        q_send[p, 1] = ktile
    live = go([
        copy(q_send.at[p % NZL], q_recv.at[z], q_ss.at[k], q_rs.at[k], dev(p, core)) for p, k in z_peers
    ])
    q_recv[z] = q_send[zl]
    done(outward)
    flat = rz_recv[...].reshape(slots, channels)
    rp_send[...] = jnp.dot(back[...], flat, preferred_element_type=F32).astype(BF16).reshape(rp_send.shape)
    outward = go([copy(rp_send.at[d], rp_recv.at[mine], o_ss.at[k], o_rs.at[k], peer) for d, peer, k in plane])
    rp_recv[mine] = rp_send[mine]
    done(live)
    both = q_recv[0]
    for q in range(1, NZ):
        both = both + q_recv[q]
    zg[zl] = both[0]
    kxg[mine] = both[1]
    live = go([copy(zg.at[zl], zg.at[zl], g_ss.at[k], g_rs.at[k], dev(p, core)) for p, k in [(zh * NZL + (zl + k) % NZL, k) for k in range(1, NZL)]])
    klive = go([copy(kxg.at[mine], kxg.at[mine], kxg_ss.at[k], kxg_rs.at[k], peer) for _, peer, k in plane])
    done(live)
    for p in range(NZL):
        r = (p // 2) * 8
        c = (p % 2) * 128
        out[r : r + 8, c : c + 128] = zg[p].astype(BF16)
    live = go([copy(out, xg.at[mine], xg_ss.at[k], xg_rs.at[k], peer) for _, peer, k in plane])
    relay = go([copy(out, cg.at[mine], cg_ss.at[0], cg_rs.at[0], partner)])
    xg[mine] = out[...]
    done(klive)
    for d in range(n):
        r, c = (d // 2) % 2 * 8, d % 2 * 128
        ko_ref[d // 4, r : r + 8, c : c + 128] = kxg[d]
    for got, (d, k) in zip(live, senders):
        got.wait_recv()
        relay += go([copy(xg.at[d], cg.at[d], cg_ss.at[k], cg_rs.at[k], partner)])
    for got in live:
        got.wait_send()
    done(outward)
    grad_ref[...] = jnp.dot(
        place[...], rp_recv[...].reshape(slots, channels), preferred_element_type=F32
    ).astype(BF16)
    for d in range(n):
        wo_ref[pl.ds(pl.multiple_of(core * half + d * prow, prow), prow)] = xg[d].astype(F32)
    done(relay)
    for d in range(n):
        wo_ref[pl.ds(pl.multiple_of((1 - core) * half + d * prow, prow), prow)] = cg[d].astype(F32)


def on_device(obs_values, obs_tile, obs_cell, backdrop, seed_grad, kernels, weights):
    spatial = lax.axis_size("lon") * lax.axis_size("lat")
    count, channels = obs_values.shape[1:]
    cap = 2 * count // spatial
    items = cap + 1
    rows, cols = backdrop.shape[1:3]
    layers = weights.shape[0]
    edge = layers
    width = cols + 16
    scale = 1.0 / float(lax.axis_size("ens") * spatial * rows * cols) ** 0.5
    group = NX * NY
    depth = layers * channels
    block = (group, depth // (NC * group), channels)
    tiles = (group, 8, 128)
    slots = cap * spatial
    V = pltpu.VMEM
    D = pltpu.SemaphoreType.DMA
    send = (group, items * NZL, channels)
    line = rows * 8
    state, w, k, grad = pl.pallas_call(
        functools.partial(whole_kernel, scale),
        out_shape=(
            jax.ShapeDtypeStruct((rows, cols, channels), BF16),
            jax.ShapeDtypeStruct((depth, channels), F32),
            jax.ShapeDtypeStruct((layers, 16, channels), F32),
            jax.ShapeDtypeStruct((count, channels), BF16),
        ),
        in_specs=[pl.BlockSpec(memory_space=V)] * 7,
        out_specs=(pl.BlockSpec(memory_space=V),) * 4,
        scratch_shapes=[
            V(send, BF16), V(send, BF16), V((items * spatial, items * spatial), BF16),
            V((NZL, items * group, channels), BF16), V((NZL, items * group, channels), BF16),
            V((rows, cols, channels), BF16), V((2, line, channels), BF16), V((2, line, channels), BF16),
            V((2, rows, cols, channels), BF16), V((2, 3, line, channels), BF16),
            V((2, edge, cols, channels), BF16), V((2, line, channels), BF16), V((2, 2, edge * 8, channels), BF16),
            V((count, slots), BF16), V((slots, slots), BF16), V((cap, spatial, rows * cols), BF16),
            V((rows * cols, channels), F32), V((layers, 3 * rows, width, channels), F32),
            V((layers, 3 * rows, width, channels), F32), V((3 * rows, width, channels), BF16),
            V((layers, rows * cols, channels), BF16), V((2 * edge + rows, width, channels), F32),
            V((2 * edge + rows, width, channels), F32), V((depth, channels), F32), V((layers, 16, channels), F32),
            V((NZL, cap * group, channels), BF16), V((NZL, cap * group, channels), BF16),
            V((group, cap * NZL, channels), BF16), V((group, cap * NZL, channels), BF16),
            V((NC,) + block, BF16), V(block, BF16), V(block, BF16), V(block, BF16),
            V((NZL, 2, 8, 128), F32), V((NZ, 2, 8, 128), F32), V((NZL, 8, 128), F32),
            V(block[1:], BF16), V(block, BF16), V(block, BF16),
            V((layers, 16, channels), F32), V(tiles, F32), V(tiles, F32), V(tiles, F32),
            D((group,)), D((group,)), D((NZL,)), D((NZL,)), D((8,)), D((8,)), D((8,)), D((8,)),
            D((NZL,)), D((NZL,)), D((group,)), D((group,)),
            D((group,)), D((group,)), D((group,)), D((group,)), D((NZ,)), D((NZ,)), D((NZL,)), D((NZL,)),
            D, D, D((group,)), D((group,)), D((group,)), D((group,)), D((group,)), D((group,)),
            D((group,)), D((group,)),
        ],
        compiler_params=pltpu.CompilerParams(
            collective_id=0, has_side_effects=True, vmem_limit_bytes=56 * 2**20
        ),
        name="window",
    )(obs_values[0], obs_tile.reshape(1, count), obs_cell, backdrop[0], seed_grad[0], kernels, weights)
    taps = kernels.shape[1]
    return state[None], w.reshape(weights.shape), k[:, :taps], grad[None]


def solution(mesh):
    placed = (
        P("ens", ("lon", "lat"), None),
        P("ens", ("lon", "lat"), None),
        P("ens", ("lon", "lat")),
        P("ens", "lat", "lon", None),
        P("ens", "lat", "lon", None),
        P(),
        P(),
    )
    return jax.shard_map(
        on_device,
        mesh=mesh,
        in_specs=placed,
        out_specs=(P("ens", "lat", "lon", None), P(), P(), P("ens", ("lon", "lat"), None)),
        check_vma=False,
    )
```

time: 141 us -> 107 us (0.76)
  other arithmetic: 12.3 us -> 0 us
  matrix products: 11.5 us -> 0 us
  starting transfers between devices: 8.79 us -> 0 us
    dot_general x14 -> x0, matrix products: 11.5 us -> none  [the longest x4 6.09 us: on_device(): lax.dot_general(acts[l], crop(grad_bf, radius).reshape(n_cells, channels)...]
    all_to_all x1 -> x0, starting transfers between devices: 8.79 us -> none  [on_device(): lax.all_to_all(slot_grad.reshape(spatial, 1, cap, channels), ('lon', 'lat...]
    convert_element_type x9 -> x0, other arithmetic: 5.65 us -> none  [the longest x4 4.08 us: on_device(): act = jax.nn.silu(pre).astype(BF16)]
    unnamed x36 -> x7, local copies, waits for them, and re-layouts: 4.94 us -> 7.44 us
    mul x1 -> x0, other arithmetic: 1.88 us -> none  [on_device(): grad = seed_wide.astype(F32) * inv_scale]
    slice x2 -> x0, local copies, waits for them, and re-layouts: 1.77 us -> none  [depthwise(): kernel_rows[3 * a + b]]
    another operation x2 -> x0, other arithmetic: 1.68 us -> none  [the longest x1 1.04 us: on_device(): jnp.stack(wgrads)]
    div x1 -> x0, other arithmetic: 1.45 us -> none  [on_device(): act = jax.nn.silu(pre).astype(BF16)]
  transfers between devices with their start and end apart: 1 -> 0, of which waited for: 0 -> 0; matrix products, arithmetic and copies ran while one was open for 10% -> 0% of each run, Pallas kernels for 37% -> 0%
where the time goes in v4:
time: 107 us; the launch traced here: 106 us
  Pallas kernels  98.2 us (92%)
  local copies, waits for them, and re-layouts  7.44 us (7%)
    pallas_call x1, Pallas kernels, on_device(): pl.pallas_call(functools.partial(whole_kernel, scale), out_shape=(jax.Sha...  98.2 us
    unnamed x7, local copies, waits for them, and re-layouts  7.44 us

profile of v4, /device:TPU:1, one launch (start us, length us, event | category | flops | bytes accessed | tf_op | source)
XLA Modules:
  0.0 106.3 jit_solution(15516745759370139592)
XLA Ops:
  0.6 1.4 %copy.11.k_ref = f32[4,9,256]{2,1,0:T(8,128)} copy(f32[4,9,256]{2,0,1:T(4,128)} %param.12) | data formatting | bytes 73728 | tf_op args[5]
  2.0 98.2 %window.1 = (bf16[8,32,256]{2,1,0:T(8,128)(2,1)}, f32[1024,256]{1,0:T(8,128)}, f32[4,16,256]{2,1,0:T(8,128)}, bf16[256,256]{1,0:T(8,128)(2,1)}) custom-call(bf16[256,256]{1,0:T(8,128)(2,1)} %bitcast.9, s32[1,256]{1,0:T(1,128)} %bitcast.15, s32[1,256]{1,0:T(1,128)} %cell_ref.1, bf16[8,32,256]{2,1,0:T(8,128)(2,1)} %bitcast.10, bf16[8,32,256]{2,1,0:T(8,128)(2,1)} %bitcast.11, ...), custom_call_target="tpu_custom_call" | custom-call | tf_op jit(solution)/shard_map/window/pallas_call | solution.py:409
  100.3 1.5 %copy.12 = f32[4,9,256]{2,0,1:T(4,128)} copy(f32[4,9,256]{2,1,0:T(8,128)} %bitcast.14) | data formatting | bytes 73728
  101.8 1.6 %copy.16 = bf16[1,8,32,256]{3,2,1,0:T(8,128)(2,1)} copy(bf16[1,8,32,256]{3,2,1,0:T(8,128)(2,1)} %bitcast.13) | data formatting | bytes 262144
  103.3 0.0 copy-start
  103.3 2.3 %copy.17 = f32[4,256,256]{2,1,0:T(8,128)} copy(f32[4,256,256]{2,1,0:T(8,128)} %bitcast.8) | data formatting | bytes 2097152
  105.7 0.0 copy-done
  105.7 0.7 copy.18
Async XLA Ops:
  103.3 2.3 %copy-start = (bf16[256,256]{1,0:T(8,128)(2,1)S(1)}, bf16[256,256]{1,0:T(8,128)(2,1)}, u32[]{:S(2)}) copy-start(bf16[256,256]{1,0:T(8,128)(2,1)} %get-tuple-element.11) | copy-start | bytes 393220

commit v5 on v4

--- a/solution.py
+++ b/solution.py
@@ -224,7 +224,7 @@
 
     for l in range(layers):
         lo, hi = l + 1, tall - 1 - l
-        taps = [k_ref[l, t : t + 1] for t in range(9)]
+        taps = [k_ref[t, l : l + 1] for t in range(9)]
 
         def forward(p, _, l=l, taps=taps):
             lines = [hs[l, p + a - 1] for a in range(3)]
@@ -254,6 +254,31 @@
 
             lax.fori_loop(0, 2, mix, 0)
     shift = rows - edge
+    prow = c_send.shape[1]
+    half = channels // NC
+
+    def rows_of(d, c):
+        start = d // 4 * channels + c * half + d % 4 * prow
+        return pl.ds(pl.multiple_of(start, prow), prow)
+
+    def swap(d):
+        return copy(c_send.at[d], c_recv.at[d], c_ss.at[d], c_rs.at[d], partner)
+
+    def hand(l):
+        for d in range(4 * l, 4 * l + 4):
+            c_send[d] = wg[rows_of(d, 1 - core)].astype(BF16)
+            swap(d).start()
+
+    def push(l):
+        for d in range(4 * l, 4 * l + 4):
+            swap(d).wait()
+            x_send[d] = (wg[rows_of(d, core)] + c_recv[d].astype(F32)).astype(BF16)
+
+            @pl.when(mine != d)
+            def _(d=d):
+                to_peer = at(zl * NY + d // NX, d % NX)
+                copy(x_send.at[d], x_recv.at[mine], x_ss.at[d], x_rs.at[mine], to_peer).start()
+
     for l in reversed(range(layers)):
         radius = l + 1
         lo, hi = edge - radius, edge + rows + radius
@@ -276,6 +301,9 @@
         wg[l * channels : (l + 1) * channels] = lax.dot_general(
             own[l], g_own, (((0,), (0,)), ((), ())), preferred_element_type=F32
         )
+        hand(l)
+        if l + 1 < layers:
+            push(l + 1)
         col = lax.broadcasted_iota(jnp.int32, (width, channels), 0)
         mid = (col >= 8) & (col < 8 + cols)
 
@@ -291,7 +319,7 @@
         acc = lax.fori_loop(0, rows, tap_sums, tuple(jnp.zeros((8, channels), F32) for _ in range(9)))
         lines = [jnp.sum(v, axis=0, keepdims=True) for v in acc]
         kg[l] = jnp.concatenate(lines + [jnp.zeros((kg.shape[1] - 9, channels), F32)], axis=0)
-        taps = [k_ref[l, t : t + 1] for t in range(9)]
+        taps = [k_ref[t, l : l + 1] for t in range(9)]
 
         def spread(q, _, taps=taps):
             lines = [es[q + 1 - a] for a in range(3)]
@@ -311,12 +339,9 @@
     for k in range(1, NX * NY):
         px, py = (x + NX - k % NX) % NX, (y + NY - k // NX) % NY
         senders.append((py * NX + px, k))
-    n, prow = c_send.shape[1], c_send.shape[2]
-    half = n * prow
-    c_send[...] = wg[...].astype(BF16).reshape(c_send.shape)
-    order = [(d, k) for d, _, k in plane] + [(mine, 0)]
+    n = c_send.shape[0]
     first = go([copy(kg, kc_recv, kc_ss, kc_rs, partner)])
-    pieces = go([copy(c_send.at[1 - core, d], c_recv.at[d], c_ss.at[k], c_rs.at[k], partner) for d, k in order])
+    push(0)
     done(first)
     ksum = kg[...] + kc_recv[...]
     for d in range(n):
@@ -324,15 +349,8 @@
         kx_send[d] = ksum[d // 4, r : r + 8, c : c + 128]
     live = go([copy(kx_send.at[d], kx_recv.at[mine], kx_ss.at[k], kx_rs.at[k], peer) for d, peer, k in plane])
     kx_recv[mine] = kx_send[mine]
-    for (d, k), piece in zip(order, pieces):
-        piece.wait_recv()
-        own = wg[pl.ds(pl.multiple_of(core * half + d * prow, prow), prow)]
-        x_send[d] = (own + c_recv[d].astype(F32)).astype(BF16)
-        if k:
-            live += go([copy(x_send.at[d], x_recv.at[mine], x_ss.at[k], x_rs.at[k], plane[k - 1][1])])
     x_recv[mine] = x_send[mine]
-    for piece in pieces:
-        piece.wait_send()
+    live += [copy(x_send.at[d], x_recv.at[d], x_ss.at[d], x_rs.at[d], peer) for d, peer, _ in plane]
     done(live)
     total = x_recv[0].astype(F32)
     ktile = kx_recv[0]
@@ -381,10 +399,10 @@
         place[...], rp_recv[...].reshape(slots, channels), preferred_element_type=F32
     ).astype(BF16)
     for d in range(n):
-        wo_ref[pl.ds(pl.multiple_of(core * half + d * prow, prow), prow)] = xg[d].astype(F32)
+        wo_ref[rows_of(d, core)] = xg[d]
     done(relay)
     for d in range(n):
-        wo_ref[pl.ds(pl.multiple_of((1 - core) * half + d * prow, prow), prow)] = cg[d].astype(F32)
+        wo_ref[rows_of(d, 1 - core)] = cg[d]
 
 
 def on_device(obs_values, obs_tile, obs_cell, backdrop, seed_grad, kernels, weights):
@@ -410,7 +428,7 @@
         functools.partial(whole_kernel, scale),
         out_shape=(
             jax.ShapeDtypeStruct((rows, cols, channels), BF16),
-            jax.ShapeDtypeStruct((depth, channels), F32),
+            jax.ShapeDtypeStruct((depth, channels), BF16),
             jax.ShapeDtypeStruct((layers, 16, channels), F32),
             jax.ShapeDtypeStruct((count, channels), BF16),
         ),
@@ -429,7 +447,7 @@
             V((2 * edge + rows, width, channels), F32), V((depth, channels), F32), V((layers, 16, channels), F32),
             V((NZL, cap * group, channels), BF16), V((NZL, cap * group, channels), BF16),
             V((group, cap * NZL, channels), BF16), V((group, cap * NZL, channels), BF16),
-            V((NC,) + block, BF16), V(block, BF16), V(block, BF16), V(block, BF16),
+            V(block, BF16), V(block, BF16), V(block, BF16), V(block, BF16),
             V((NZL, 2, 8, 128), F32), V((NZ, 2, 8, 128), F32), V((NZL, 8, 128), F32),
             V(block[1:], BF16), V(block, BF16), V(block, BF16),
             V((layers, 16, channels), F32), V(tiles, F32), V(tiles, F32), V(tiles, F32),
@@ -443,9 +461,9 @@
             collective_id=0, has_side_effects=True, vmem_limit_bytes=56 * 2**20
         ),
         name="window",
-    )(obs_values[0], obs_tile.reshape(1, count), obs_cell, backdrop[0], seed_grad[0], kernels, weights)
+    )(obs_values[0], obs_tile.reshape(1, count), obs_cell, backdrop[0], seed_grad[0], kernels.transpose(1, 0, 2), weights)
     taps = kernels.shape[1]
-    return state[None], w.reshape(weights.shape), k[:, :taps], grad[None]
+    return state[None], w.reshape(weights.shape).astype(F32), k[:, :taps], grad[None]
 
 
 def solution(mesh):

time: 107 us -> 104 us (0.972)
  local copies, waits for them, and re-layouts: 7.44 us -> 3.09 us
  other arithmetic: 0 us -> 2.13 us
    unnamed x7, local copies, waits for them, and re-layouts: 7.44 us -> 3.09 us
    convert_element_type x0 -> x1, other arithmetic: none -> 2.13 us  [on_device(): w.reshape(weights.shape).astype(F32)]
where the time goes in v5:
time: 104 us
  Pallas kernels  98.3 us (95%)
  local copies, waits for them, and re-layouts  3.09 us (3%)
  other arithmetic  2.13 us (2%)
    pallas_call x1, Pallas kernels, on_device(): pl.pallas_call(functools.partial(whole_kernel, scale), out_shape=(jax.Sha...  98.3 us
    unnamed x7, local copies, waits for them, and re-layouts  3.09 us
    convert_element_type x1, other arithmetic, on_device(): w.reshape(weights.shape).astype(F32)  2.13 us

profile of v5, /device:TPU:1, one launch (start us, length us, event | category | flops | bytes accessed | tf_op | source)
XLA Modules:
  0.0 104.1 jit_solution(15646357651929696470)
XLA Ops:
  0.6 98.3 %window.1 = (bf16[8,32,256]{2,1,0:T(8,128)(2,1)}, bf16[1024,256]{1,0:T(8,128)(2,1)}, f32[4,16,256]{2,1,0:T(8,128)}, bf16[256,256]{1,0:T(8,128)(2,1)}) custom-call(bf16[256,256]{1,0:T(8,128)(2,1)} %bitcast.13, s32[1,256]{1,0:T(1,128)} %bitcast.18, s32[1,256]{1,0:T(1,128)} %cell_ref.1, bf16[8,32,256]{2,1,0:T(8,128)(2,1)} %bitcast.14, ...), custom_call_target="tpu_custom_call" | custom-call | tf_op jit(solution)/shard_map/window/pallas_call | solution.py:427
  98.9 1.5 %copy.11 = f32[4,9,256]{2,0,1:T(4,128)} copy(f32[4,9,256]{2,1,0:T(8,128)} %bitcast.16) | data formatting | bytes 73728
  100.4 0.0 copy-start.1
  100.4 2.1 %convert.1 = f32[4,256,256]{2,1,0:T(8,128)} convert(bf16[4,256,256]{2,1,0:T(8,128)(2,1)} %bitcast.10) | non-fusion elementwise | flops 262144 | bytes 1572864 | tf_op jit(solution)/shard_map/convert_element_type | solution.py:466
  102.5 0.0 copy-done.1
  102.5 0.0 copy-start
  102.5 0.7 copy.14
  103.2 0.3 copy-done
  103.5 0.7 copy.15
Async XLA Ops:
  100.4 2.1 %copy-start.1 = (bf16[8,32,256]{2,1,0:T(8,128)(2,1)S(1)}, bf16[8,32,256]{2,1,0:T(8,128)(2,1)}, u32[]{:S(2)}) copy-start(bf16[8,32,256]{2,1,0:T(8,128)(2,1)} %get-tuple-element.8) | copy-start | bytes 393220
  102.5 1.0 copy-start

commit v6 on v5

--- a/solution.py
+++ b/solution.py
@@ -143,7 +143,6 @@
             copy(src, s_mid.at[side], s_ss.at[n + 1], s_rs.at[n + 1], at(other, x)),
             copy(src.at[0:cut], s_end.at[side, 1], s_ss.at[n + 2], s_rs.at[n + 2], at(other, north)),
         ]
-    go(seeds)
     r1[mine] = send_ref[mine]
     done(live)
     flat = r1[...].astype(F32).reshape(total, channels).astype(BF16)
@@ -151,6 +150,7 @@
         jnp.dot(perm[...], flat, preferred_element_type=F32).astype(BF16).reshape(z_send.shape)
     )
     live = go([copy(z_send.at[p], r2.at[zl], z_ss.at[k], z_rs.at[k], peer) for p, peer, k in along])
+    go(seeds)
     r2[zl] = z_send[zl]
     done(live)
     n_cells = rows * cols

time: 104 us -> 105 us (level)
  no operation moved by 1% of the time
where the time goes in v6:
time: 105 us
  Pallas kernels  99.3 us (95%)
  local copies, waits for them, and re-layouts  3.09 us (3%)
  other arithmetic  2.13 us (2%)
    pallas_call x1, Pallas kernels, on_device(): pl.pallas_call(functools.partial(whole_kernel, scale), out_shape=(jax.Sha...  99.3 us
    unnamed x7, local copies, waits for them, and re-layouts  3.09 us
    convert_element_type x1, other arithmetic, on_device(): w.reshape(weights.shape).astype(F32)  2.13 us

profile of v6, /device:TPU:1, one launch (start us, length us, event | category | flops | bytes accessed | tf_op | source)
XLA Modules:
  0.0 105.1 jit_solution(6907426416771518630)
XLA Ops:
  0.6 99.3 %window.1 = (bf16[8,32,256]{2,1,0:T(8,128)(2,1)}, bf16[1024,256]{1,0:T(8,128)(2,1)}, f32[4,16,256]{2,1,0:T(8,128)}, bf16[256,256]{1,0:T(8,128)(2,1)}) custom-call(bf16[256,256]{1,0:T(8,128)(2,1)} %bitcast.13, s32[1,256]{1,0:T(1,128)} %bitcast.18, s32[1,256]{1,0:T(1,128)} %cell_ref.1, bf16[8,32,256]{2,1,0:T(8,128)(2,1)} %bitcast.14, ...), custom_call_target="tpu_custom_call" | custom-call | tf_op jit(solution)/shard_map/window/pallas_call | solution.py:427
  99.9 1.5 %copy.11 = f32[4,9,256]{2,0,1:T(4,128)} copy(f32[4,9,256]{2,1,0:T(8,128)} %bitcast.16) | data formatting | bytes 73728
  101.4 0.0 copy-start.1
  101.4 2.1 %convert.1 = f32[4,256,256]{2,1,0:T(8,128)} convert(bf16[4,256,256]{2,1,0:T(8,128)(2,1)} %bitcast.10) | non-fusion elementwise | flops 262144 | bytes 1572864 | tf_op jit(solution)/shard_map/convert_element_type | solution.py:466
  103.5 0.0 copy-done.1
  103.5 0.0 copy-start
  103.5 0.7 copy.14
  104.2 0.3 copy-done
  104.5 0.7 copy.15
Async XLA Ops:
  101.4 2.1 %copy-start.1 = (bf16[8,32,256]{2,1,0:T(8,128)(2,1)S(1)}, bf16[8,32,256]{2,1,0:T(8,128)(2,1)}, u32[]{:S(2)}) copy-start(bf16[8,32,256]{2,1,0:T(8,128)(2,1)} %get-tuple-element.8) | copy-start | bytes 393220
  103.5 1.0 copy-start
